TPU v7x, 256 devices: a whole 4x4x8 slice. The times are simulated.
256 devices in a mesh: seq: 32 (over y, z), head: 8 (over x, core).
Axes of the slice: x: 4, y: 4, z: 8, core: 2. Of those that a mesh axis runs over, the one named last changes fastest.
Arguments:
- new_query: bfloat16 [96, 4, 4096], P(None, None, 'head'), may hold values from -40 to 40
- fresh_key_value: bfloat16 [96, 4, 8, 128], P('seq', None, 'head'), may hold values from -24 to 24
- prompt_cache: bfloat16 [8, 32768, 8, 128], P(None, 'seq', 'head'), may hold values from -30 to 30
- decoded_tail_cache: bfloat16 [96, 1024, 8, 128], P(None, 'seq', 'head'), may hold values from -6 to 6
- sinks: float32 [64], P('head'), may hold values from 2 to 14
- prompt_group: int32 [96], replicated, may hold values from 0 to 7, as said below
- prompt_lens: int32 [8], replicated, may hold values from 1 to 32768
- tail_lens: int32 [96], replicated, may hold values from 0 to 1024
- o_weight: bfloat16 [4096, 2880], P('head'), may hold values from -0.09375 to 0.09375
- resid: bfloat16 [96, 4, 2880], P('seq'), may hold values from -1.796875 to 1.796875
- norm_gain: float32 [2880], replicated, may hold values from 0.3 to 3
- expert_ids: int32 [96, 4, 4], replicated, may hold values from 0 to 31, all different within a row; in each aligned block of 12 rows (0 to 11, 12 to 23, ..., all dimensions but the last counted through in order) at most 3 rows name the same one
- route_weights: float32 [96, 4, 4], P('seq'), may hold values from 0.05 to 0.6
- gate_up: bfloat16 [32, 2880, 2, 2880], P('seq', None, None, 'head'), may hold values from -0.3125 to 0.3125
- down_weight: bfloat16 [32, 2880, 2880], P('seq', 'head'), may hold values from -0.0390625 to 0.0390625
Outputs:
- output: bfloat16 [96, 4, 2880], P('seq')
Inputs may be any that keep to these rules, and one draw needn't show every extreme that they name: `prompt_group`: each of the 8 groups holds exactly 12 requests. `expert_ids`: a token's 4 picks are distinct; among the 12 tokens of the requests s * 3 to (s + 1) * 3 - 1 no expert is picked more than 3 times.
All inputs are finite; a program needn't handle non-finite values.
Results may differ from a plain program's by a relative error of at most 0.025.
Values may be sent and summed in bfloat16 or wider, within the bound.
A program may use at most 128 MiB of HBM per device.

v0:
```python
import math

import jax
import jax.numpy as jnp
from jax import lax
from jax.sharding import PartitionSpec as P

very_low = -1e30


def rotate(vector, position):
    half_width = vector.shape[-1] // 2
    frequency = jnp.exp(
        jnp.arange(half_width, dtype=jnp.float32) * (-2.0 * math.log(150000.0) / vector.shape[-1])
    )
    angle = position[..., None] * frequency
    cosine = jnp.cos(angle)
    sine_part = jnp.sin(angle)
    leading = vector[..., :half_width]
    trailing = vector[..., half_width:]
    return jnp.concatenate(
        [leading * cosine - trailing * sine_part, trailing * cosine + leading * sine_part], axis=-1
    )


def block_weights(scores, valid):
    masked = jnp.where(valid, scores, very_low)
    highest = jnp.max(masked, axis=-1)
    weights = jnp.where(valid, jnp.exp(masked - highest[..., None]), 0.0)
    return (highest, jnp.sum(weights, axis=-1), weights)


def joined_stats(first, second):
    highest_a, total_a, weighted_a = first
    highest_b, total_b, weighted_b = second
    highest = jnp.maximum(highest_a, highest_b)
    factor_a = jnp.exp(highest_a - highest)
    factor_b = jnp.exp(highest_b - highest)
    spread_count = weighted_a.shape[-1] // highest_a.shape[-1]
    weighted = weighted_a * jnp.repeat(factor_a, spread_count, axis=-1) + weighted_b * jnp.repeat(
        factor_b, spread_count, axis=-1
    )
    return (highest, total_a * factor_a + total_b * factor_b, weighted)


def slot_numbers(picks, experts_total):
    one_hot = (picks[..., None] == jnp.arange(experts_total, dtype=jnp.int32)).astype(jnp.int32)
    earlier = jnp.cumsum(one_hot, axis=-2) - one_hot
    return jnp.sum(earlier * one_hot, axis=-1)


def on_device(
    new_query,
    fresh_key_value,
    prompt_cache,
    decoded_tail_cache,
    sinks,
    prompt_group,
    prompt_lens,
    tail_lens,
    o_weight,
    resid,
    norm_gain,
    expert_ids,
    route_weights,
    gate_up,
    down_weight,
):
    seq_count = lax.axis_size("seq")
    seq_index = lax.axis_index("seq")
    groups_total, prompt_block, kv_local, double_width = prompt_cache.shape
    head_dim = double_width // 2
    requests, steps_total, query_width = new_query.shape
    heads_local = query_width // head_dim
    requests_per_group = heads_local // kv_local
    owned = fresh_key_value.shape[0]
    tail_block = decoded_tail_cache.shape[1]
    group_size = requests // groups_total
    model_width = resid.shape[-1]
    factor_scale = 1.0 / math.sqrt(head_dim)
    first_row = seq_index * owned
    group_hot = prompt_group[:, None] == jnp.arange(groups_total, dtype=jnp.int32)[None, :]
    prompt_start = jnp.sum(jnp.where(group_hot, prompt_lens[None, :], 0), axis=1)
    positions = (
        (prompt_start + tail_lens)[:, None] + jnp.arange(steps_total, dtype=jnp.int32)[None, :]
    ).astype(jnp.float32)
    query_matrix = new_query.reshape(requests, steps_total, heads_local, head_dim).astype(
        jnp.float32
    )
    rotated = rotate(query_matrix, positions[:, :, None]).astype(jnp.bfloat16)
    rotated = rotated.reshape(requests, steps_total, kv_local, requests_per_group, head_dim)
    ordering = jnp.argsort(prompt_group, stable=True)
    inverse = jnp.zeros_like(ordering).at[ordering].set(jnp.arange(requests, dtype=jnp.int32))
    grouped = rotated[ordering].reshape(
        groups_total, group_size, steps_total, kv_local, requests_per_group, head_dim
    )
    prompt_scores = (
        jnp.einsum(
            "grtcjd,gpcd->grtcjp",
            grouped,
            prompt_cache[..., :head_dim],
            preferred_element_type=jnp.float32,
        )
        * factor_scale
    )
    prompt_valid = (seq_index * prompt_block + jnp.arange(prompt_block, dtype=jnp.int32))[
        None, :
    ] < prompt_lens[:, None]
    prompt_high, prompt_total, prompt_weights = block_weights(
        prompt_scores, prompt_valid[:, None, None, None, None, :]
    )
    prompt_acc = jnp.einsum(
        "grtcjp,gpcd->grtcjd",
        prompt_weights.astype(jnp.bfloat16),
        prompt_cache[..., head_dim:],
        preferred_element_type=jnp.float32,
    )
    prompt_stats = (
        prompt_high.reshape(requests, steps_total, heads_local)[inverse],
        prompt_total.reshape(requests, steps_total, heads_local)[inverse],
        prompt_acc.reshape(requests, steps_total, query_width)[inverse],
    )
    tail_scores = (
        jnp.einsum(
            "rtcjd,rucd->rtcju",
            rotated,
            decoded_tail_cache[..., :head_dim],
            preferred_element_type=jnp.float32,
        )
        * factor_scale
    )
    tail_valid = (seq_index * tail_block + jnp.arange(tail_block, dtype=jnp.int32))[
        None, :
    ] < tail_lens[:, None]
    tail_high, tail_total, tail_weights = block_weights(
        tail_scores, tail_valid[:, None, None, None, :]
    )
    tail_acc = jnp.einsum(
        "rtcju,rucd->rtcjd",
        tail_weights.astype(jnp.bfloat16),
        decoded_tail_cache[..., head_dim:],
        preferred_element_type=jnp.float32,
    )
    tail_stats = (
        tail_high.reshape(requests, steps_total, heads_local),
        tail_total.reshape(requests, steps_total, heads_local),
        tail_acc.reshape(requests, steps_total, query_width),
    )
    local_stats = joined_stats(prompt_stats, tail_stats)
    own_query = lax.dynamic_slice_in_dim(rotated, first_row, owned, 0)
    own_positions = lax.dynamic_slice_in_dim(positions, first_row, owned, 0)
    fresh_keys = rotate(
        fresh_key_value[..., :head_dim].astype(jnp.float32), own_positions[:, :, None]
    ).astype(jnp.bfloat16)
    fresh_scores = (
        jnp.einsum("rtcjd,rucd->rtcju", own_query, fresh_keys, preferred_element_type=jnp.float32)
        * factor_scale
    )
    causal = jnp.arange(steps_total)[None, :] <= jnp.arange(steps_total)[:, None]
    fresh_high, fresh_total, fresh_weights = block_weights(
        fresh_scores, causal[None, :, None, None, :]
    )
    fresh_acc = jnp.einsum(
        "rtcju,rucd->rtcjd",
        fresh_weights.astype(jnp.bfloat16),
        fresh_key_value[..., head_dim:],
        preferred_element_type=jnp.float32,
    )
    fresh_stats = (
        fresh_high.reshape(owned, steps_total, heads_local),
        fresh_total.reshape(owned, steps_total, heads_local),
        fresh_acc.reshape(owned, steps_total, query_width),
    )
    by_owner = tuple(
        (member.reshape((seq_count, owned) + member.shape[1:]) for member in local_stats)
    )
    recv_high, recv_total, recv_acc = (
        lax.all_to_all(by_owner[0], "seq", split_axis=0, concat_axis=0, tiled=True),
        lax.all_to_all(by_owner[1], "seq", split_axis=0, concat_axis=0, tiled=True),
        lax.all_to_all(by_owner[2], "seq", split_axis=0, concat_axis=0, tiled=True),
    )
    owner_high = jnp.max(recv_high, axis=0)
    factors = jnp.exp(recv_high - owner_high[None])
    owner_total = jnp.sum(recv_total * factors, axis=0)
    owner_acc = jnp.sum(recv_acc * jnp.repeat(factors, head_dim, axis=-1), axis=0)
    final_stats = joined_stats((owner_high, owner_total, owner_acc), fresh_stats)
    final_high, final_total, final_acc = final_stats
    with_sink = jnp.maximum(final_high, sinks)
    kept = jnp.exp(final_high - with_sink)
    denom_total = final_total * kept + jnp.exp(sinks - with_sink)
    attended = (final_acc * jnp.repeat(kept / denom_total, head_dim, axis=-1)).astype(jnp.bfloat16)
    token_count = owned * steps_total
    partial_proj = jnp.dot(
        attended.reshape(token_count, query_width), o_weight, preferred_element_type=jnp.float32
    )
    projected = lax.psum(partial_proj, "head")
    hidden = (resid.reshape(token_count, model_width).astype(jnp.float32) + projected).astype(
        jnp.bfloat16
    )
    wide = hidden.astype(jnp.float32)
    normed = (
        wide * lax.rsqrt(jnp.mean(wide * wide, axis=-1, keepdims=True) + 1e-05) * norm_gain
    ).astype(jnp.bfloat16)
    experts_local = gate_up.shape[0]
    hidden_local = gate_up.shape[-1]
    experts_total = experts_local * seq_count
    top_count = expert_ids.shape[-1]
    capacity = token_count * top_count // experts_total + 2
    pair_count = token_count * top_count
    all_picks = expert_ids.reshape(seq_count, pair_count)
    own_picks = lax.dynamic_slice_in_dim(all_picks, seq_index, 1, 0)[0]
    own_index = own_picks * capacity + slot_numbers(own_picks, experts_total)
    pair_token = jnp.arange(pair_count, dtype=jnp.int32) // top_count
    joined_weight = gate_up.reshape(experts_local, model_width, 2 * hidden_local)
    outgoing = (
        jnp.zeros((experts_total * capacity, model_width), jnp.bfloat16)
        .at[own_index]
        .set(normed[pair_token])
    )
    outgoing = outgoing.reshape(seq_count, experts_local, capacity, model_width)
    projected_rows = jnp.einsum(
        "nekd,edf->nekf",
        lax.all_to_all(outgoing, "seq", split_axis=0, concat_axis=0, tiled=True),
        joined_weight,
        preferred_element_type=jnp.float32,
    )
    gate_part = jnp.minimum(projected_rows[..., :hidden_local], 7.0)
    up_part = jnp.clip(projected_rows[..., hidden_local:], -7.0, 7.0)
    activation = ((up_part + 1.0) * gate_part * jax.nn.sigmoid(1.702 * gate_part)).astype(
        jnp.bfloat16
    )
    returned = lax.all_to_all(
        jnp.einsum("nekf,efd->nekd", activation, down_weight, preferred_element_type=jnp.float32),
        "seq",
        split_axis=0,
        concat_axis=0,
        tiled=True,
    )
    back_rows = returned.reshape(experts_total * capacity, model_width)[own_index]
    weighted = back_rows.reshape(token_count, top_count, model_width) * route_weights.reshape(
        token_count, top_count, 1
    )
    expert_part = jnp.sum(weighted, axis=1)
    expert_total = lax.psum(expert_part, "head")
    return (wide + expert_total).astype(jnp.bfloat16).reshape(owned, steps_total, model_width)


def solution(mesh):
    return jax.shard_map(
        on_device,
        mesh=mesh,
        in_specs=(
            P(None, None, "head"),
            P("seq", None, "head", None),
            P(None, "seq", "head", None),
            P(None, "seq", "head", None),
            P("head"),
            P(),
            P(),
            P(),
            P("head", None),
            P("seq", None, None),
            P(),
            P(),
            P("seq", None, None),
            P("seq", None, None, "head"),
            P("seq", "head", None),
        ),
        out_specs=P("seq", None, None),
        check_vma=False,
    )
```

profile of v0, /device:TPU:1, one launch (start us, length us, event | category | flops | bytes accessed | tf_op | source)
XLA Modules:
  0.0 367.5 jit_solution(5805711957272378757)
XLA Ops:
  7.5 3.2 sort.17
  16.9 3.4 copy.153
  29.1 2.7 gather_fusion
  31.8 3.7 %fusion.1 = (f32[8,12,4,8]{3,2,1,0:T(4,128)S(1)}, f32[8,12,4,8,1024]{4,3,2,1,0:T(8,128)S(1)}) fusion(pred[8,1024]{1,0:T(8,128)(4,1)S(1)} %broadcast_compare_fusion.1, bf16[8,12,4,8,64]{4,3,2,1,0:T(8,128)(2,1)} %bitcast.215, bf16[8,1024,1,128]{3,1,2,0:T(8,128)(2,1)} %param.17), kind=kOutput, calls=%fused_computation.11 | convolution fusion | flops 412087296 | bytes 15093760 | tf_op jit(solution)/shard_map/grtcjd,gpcd->grtcjp/dot_general | solution.py:98
  35.6 4.0 %fusion.2 = f32[8,12,4,8]{3,2,1,0:T(4,128)S(1)} fusion(f32[8,12,4,8,1024]{4,3,2,1,0:T(8,128)S(1)} %get-tuple-element.29, f32[8,12,4,8]{3,2,1,0:T(4,128)S(1)} %get-tuple-element.28, pred[8,1024]{1,0:T(8,128)(4,1)S(1)} %broadcast_compare_fusion.1), kind=kLoop, calls=%fused_computation.12 | loop fusion | flops 15725568 | bytes 12615680 | tf_op jit(solution)/shard_map/reduce_sum | solution.py:30
  48.0 12.3 %all-to-all-start.2 = ((f32[32,3,4,8]{3,2,1,0:T(4,128)}), f32[32,3,4,8]{3,2,1,0:T(4,128)}, u32[]{:S(2)}, u32[]{:S(2)}) async-start(f32[32,3,4,8]{3,2,1,0:T(4,128)} %get-tuple-element.11), calls=%async_computation.2 | async-start | bytes 393216 | tf_op jit(solution)/shard_map/all_to_all | solution.py:179
  61.1 3.8 %convolution_bitcast_fusion.1 = f32[96,4,1,8,64]{4,3,1,0,2:T(8,128)} fusion(f32[96,4,1,8,32]{4,3,1,0,2:T(8,128)} %copy-done.4, bf16[96,32,1,128]{3,1,0,2:T(8,128)(2,1)} %bitcast.224, f32[96,4,8]{2,1,0:T(4,128)S(1)} %get-tuple-element.26, pred[96,32]{1,0:T(8,128)(4,1)} %broadcast_compare_fusion), kind=kOutput, calls=%fused_computation.30 | convolution fusion | flops 12877824 | bytes 1981440 | tf_op jit(solution)/shard_map/rtcju,rucd->rtcjd/dot_general | solution.py:138
  65.5 9.5 %fusion.16 = f32[8,12,4,1,8,64]{5,4,2,1,0,3:T(8,128)} fusion(bf16[8,1024,1,128]{3,1,2,0:T(8,128)(2,1)} %param.17, f32[8,12,4,8,1024]{4,3,2,1,0:T(8,128)} %copy-done.1, f32[8,12,4,8]{3,2,1,0:T(4,128)S(1)} %get-tuple-element.28, pred[8,1024]{1,0:T(8,128)(4,1)S(1)} %broadcast_compare_fusion.1), kind=kOutput, calls=%fused_computation.31 | convolution fusion | flops 418381824 | bytes 15679488 | tf_op jit(solution)/shard_map/grtcjp,gpcd->grtcjd/dot_general | solution.py:112
  81.6 3.2 gather_fusion.1
  93.4 3.2 multiply_add_fusion
  96.6 9.0 %all-to-all-start.1 = ((f32[32,3,4,8]{3,2,1,0:T(4,128)}), f32[32,3,4,8]{3,2,1,0:T(4,128)S(1)}, u32[]{:S(2)}, u32[]{:S(2)}) async-start(f32[32,3,4,8]{3,2,1,0:T(4,128)} %get-tuple-element.12), calls=%async_computation.1 | async-start | bytes 393216 | tf_op jit(solution)/shard_map/all_to_all | solution.py:178
  106.3 8.7 %all-to-all-done.1 = f32[32,3,4,8]{3,2,1,0:T(4,128)S(1)} async-done(((f32[32,3,4,8]{3,2,1,0:T(4,128)}), f32[32,3,4,8]{3,2,1,0:T(4,128)S(1)}, u32[]{:S(2)}, u32[]{:S(2)}) %all-to-all-start.1) | async-done | bytes 12320 | tf_op jit(solution)/shard_map/all_to_all | solution.py:178
  115.0 4.6 %all-to-all-start = ((f32[32,3,4,512]{3,2,1,0:T(4,128)}), f32[32,3,4,512]{3,2,1,0:T(4,128)}, u32[]{:S(2)}, u32[]{:S(2)}) async-start(f32[32,3,4,512]{3,2,1,0:T(4,128)} %multiply_add_fusion), calls=%async_computation | async-start | bytes 1572864 | tf_op jit(solution)/shard_map/all_to_all | solution.py:180
  128.2 2.7 reshape.444
  130.9 5.6 %all-to-all-done = f32[32,3,4,512]{3,2,1,0:T(4,128)} async-done(((f32[32,3,4,512]{3,2,1,0:T(4,128)}), f32[32,3,4,512]{3,2,1,0:T(4,128)}, u32[]{:S(2)}, u32[]{:S(2)}) %all-to-all-start) | async-done | bytes 786464 | tf_op jit(solution)/shard_map/all_to_all | solution.py:180
  139.8 65.8 %all-reduce.3.cloned.1.call-done = f32[12,2880]{1,0:T(8,128)} async-done(((f32[12,2880]{1,0:T(8,128)}), f32[12,2880]{1,0:T(8,128)}) %all-reduce.3.cloned.1.call-update) | async-done | bytes 138256 | tf_op jit(solution)/shard_map/psum | solution.py:196
  208.0 2.9 scatter_custom_fusion.1
  212.0 25.1 %all_to_all.25 = bf16[32,1,3,2880]{3,2,1,0:T(4,128)(2,1)S(1)} all-to-all(bf16[32,1,3,2880]{3,2,1,0:T(4,128)(2,1)} %bitcast.220), channel_id=1, replica_groups=mesh['seq'=32,'head'=8] {'seq'}, dimensions={0} | all-to-all | bytes 1105920 | tf_op jit(solution)/shard_map/all_to_all | solution.py:223
  237.1 3.7 %convolution_bitcast_fusion.2 = f32[32,1,3,720]{3,0,2,1:T(8,128)S(1)} fusion(bf16[2880,720,1]{0,1,2:T(8,128)(2,1)} %bitcast.217, bf16[32,1,3,2880]{3,2,1,0:T(4,128)(2,1)S(1)} %all_to_all.25), kind=kOutput, calls=%fused_computation.34 | convolution fusion | flops 398131200 | bytes 4976640 | tf_op jit(solution)/shard_map/nekd,edf->nekf/dot_general | solution.py:221
  243.7 8.9 %all-to-all-start.4 = ((f32[32,1,3,2880]{3,1,2,0:T(1,128)}), f32[32,1,3,2880]{3,1,2,0:T(1,128)}, u32[]{:S(2)}, u32[]{:S(2)}) async-start(f32[32,1,3,2880]{3,1,2,0:T(1,128)} %copy.142), calls=%async_computation.4 | async-start | bytes 2260992 | tf_op jit(solution)/shard_map/all_to_all | solution.py:232
  252.9 22.5 %all-to-all-done.4 = f32[32,1,3,2880]{3,1,2,0:T(1,128)} async-done(((f32[32,1,3,2880]{3,1,2,0:T(1,128)}), f32[32,1,3,2880]{3,1,2,0:T(1,128)}, u32[]{:S(2)}, u32[]{:S(2)}) %all-to-all-start.4) | async-done | bytes 1105952 | tf_op jit(solution)/shard_map/all_to_all | solution.py:232
  275.4 5.5 %reduce.6 = f32[32,3,2880]{2,1,0:T(4,128)} reduce(f32[32,1,3,2880]{3,1,2,0:T(1,128)} %all-to-all-done.4, f32[]{:T(128)} %constant.78), dimensions={1}, to_apply=%all_to_all.19.reduce_sub_computation | reduce | bytes 2211844 | tf_op jit(solution)/shard_map/all_to_all | solution.py:232
  283.6 3.0 gather_fusion.4
  288.9 70.1 %all-reduce.5.cloned.1.call-done = f32[12,2880]{1,0:T(8,128)} async-done(((f32[12,2880]{1,0:T(8,128)}), f32[12,2880]{1,0:T(8,128)}) %all-reduce.5.cloned.1.call-update) | async-done | bytes 138256 | tf_op jit(solution)/shard_map/psum | solution.py:244
  (140 shorter events, 66.6 us)
Async XLA Ops:
  6.5 131.6 %copy-start = (bf16[512,2880]{0,1:T(8,128)(2,1)S(1)}, bf16[512,2880]{0,1:T(8,128)(2,1)}, u32[]{:S(2)}) copy-start(bf16[512,2880]{0,1:T(8,128)(2,1)} %param.23) | copy-start | bytes 8847364
  6.5 16.0 %copy-start.24 = (f32[32]{0:T(128)}, f32[32]{0:T(128)S(1)}, u32[]{:S(2)}) copy-start(f32[32]{0:T(128)S(1)} %multiply_exponential_fusion) | copy-start | bytes 388
  11.6 29.2 %copy-start.19 = (s32[1024]{0:T(1024)}, s32[1024]{0:T(1024)S(1)}, u32[]{:S(2)}) copy-start(s32[1024]{0:T(1024)S(1)} %pad_clamp_fusion.2) | copy-start | bytes 12292
  14.4 8.2 %copy-start.9 = (f32[96,4]{1,0:T(8,128)}, f32[96,4]{1,0:T(8,128)S(1)}, u32[]{:S(2)}) copy-start(f32[96,4]{1,0:T(8,128)S(1)} %add_convert_fusion.2) | copy-start | bytes 4612
  35.5 4.6 %copy-start.1 = (f32[8,12,4,8,1024]{4,3,2,1,0:T(8,128)}, f32[8,12,4,8,1024]{4,3,2,1,0:T(8,128)S(1)}, u32[]{:S(2)}) copy-start(f32[8,12,4,8,1024]{4,3,2,1,0:T(8,128)S(1)} %get-tuple-element.29) | copy-start | bytes 37748740
  42.2 3.8 %copy-start.11 = (pred[96,32]{1,0:T(8,128)(4,1)S(1)}, pred[96,32]{1,0:T(8,128)(4,1)}, u32[]{:S(2)}) copy-start(pred[96,32]{1,0:T(8,128)(4,1)} %broadcast_compare_fusion) | copy-start | bytes 9220
  42.2 4.9 %copy-start.8 = (f32[96,4,8]{2,1,0:T(4,128)S(1)}, f32[96,4,8]{2,1,0:T(4,128)}, u32[]{:S(2)}) copy-start(f32[96,4,8]{2,1,0:T(4,128)} %gather_fusion.3) | copy-start | bytes 36868
  48.0 48.6 %all-to-all-start.2 = ((f32[32,3,4,8]{3,2,1,0:T(4,128)}), f32[32,3,4,8]{3,2,1,0:T(4,128)}, u32[]{:S(2)}, u32[]{:S(2)}) async-start(f32[32,3,4,8]{3,2,1,0:T(4,128)} %get-tuple-element.11), calls=%async_computation.2 | async-start | bytes 393216 | tf_op jit(solution)/shard_map/all_to_all | solution.py:179
  65.5 9.5 %copy-start.18 = (s32[96,4,4]{0,2,1:T(4,128)S(1)}, s32[96,4,4]{0,2,1:T(4,128)}, u32[]{:S(2)}) copy-start(s32[96,4,4]{0,2,1:T(4,128)} %param.26) | copy-start | bytes 18436
  75.1 3.6 copy-start.13
  75.1 3.6 copy-start.14
  93.4 26.5 %copy-start.25 = (f32[32]{0:T(128)S(1)}, f32[32]{0:T(128)}, u32[]{:S(2)}) copy-start(f32[32]{0:T(128)} %copy-done.24) | copy-start | bytes 388
  93.4 26.7 %copy-start.12 = (bf16[3,4,2880]{2,1,0:T(4,128)(2,1)S(1)}, bf16[3,4,2880]{2,1,0:T(4,128)(2,1)}, u32[]{:S(2)}) copy-start(bf16[3,4,2880]{2,1,0:T(4,128)(2,1)} %param.24) | copy-start | bytes 207364
  96.6 26.2 %copy-start.22 = (s32[48]{0:T(128)S(1)}, s32[48]{0:T(128)}, u32[]{:S(2)}) copy-start(s32[48]{0:T(128)} %copy-done.21) | copy-start | bytes 580
  96.6 18.4 %all-to-all-start.1 = ((f32[32,3,4,8]{3,2,1,0:T(4,128)}), f32[32,3,4,8]{3,2,1,0:T(4,128)S(1)}, u32[]{:S(2)}, u32[]{:S(2)}) async-start(f32[32,3,4,8]{3,2,1,0:T(4,128)} %get-tuple-element.12), calls=%async_computation.1 | async-start | bytes 393216 | tf_op jit(solution)/shard_map/all_to_all | solution.py:178
  115.0 21.5 %all-to-all-start = ((f32[32,3,4,512]{3,2,1,0:T(4,128)}), f32[32,3,4,512]{3,2,1,0:T(4,128)}, u32[]{:S(2)}, u32[]{:S(2)}) async-start(f32[32,3,4,512]{3,2,1,0:T(4,128)} %multiply_add_fusion), calls=%async_computation | async-start | bytes 1572864 | tf_op jit(solution)/shard_map/all_to_all | solution.py:180
  119.7 85.9 %all-reduce.3.cloned.1.call-start = ((), (), s32[]{:S(2)}) async-start(), calls=%async_computation.5 | async-start | bytes 376832 | tf_op jit(solution)/shard_map/psum | solution.py:196
  128.2 10.0 %copy-start.10 = (f32[12,512]{1,0:T(8,128)S(1)}, f32[12,512]{1,0:T(8,128)}, u32[]{:S(2)}) copy-start(f32[12,512]{1,0:T(8,128)} %reshape.448) | copy-start | bytes 73732
  138.1 69.2 %copy-start.16 = (f32[2880]{0:T(1024)S(1)}, f32[2880]{0:T(1024)}, u32[]{:S(2)}) copy-start(f32[2880]{0:T(1024)} %param.25) | copy-start | bytes 34564
  138.2 69.8 %copy-start.23 = (s32[48]{0:T(128)S(1)}, s32[48]{0:T(128)}, u32[]{:S(2)}) copy-start(s32[48]{0:T(128)} %fusion.82) | copy-start | bytes 580
  237.1 3.8 %copy-start.5 = (bf16[1,360,2880]{2,1,0:T(8,128)(2,1)S(1)}, bf16[1,360,2880]{2,1,0:T(8,128)(2,1)}, u32[]{:S(2)}) copy-start(bf16[1,360,2880]{2,1,0:T(8,128)(2,1)} %param.29) | copy-start | bytes 6220804
  241.5 11.3 %copy-start.20 = (f32[3,4,4]{2,1,0:T(4,128)S(1)}, f32[3,4,4]{2,1,0:T(4,128)}, u32[]{:S(2)}) copy-start(f32[3,4,4]{2,1,0:T(4,128)} %param.27) | copy-start | bytes 580
  243.7 31.7 %all-to-all-start.4 = ((f32[32,1,3,2880]{3,1,2,0:T(1,128)}), f32[32,1,3,2880]{3,1,2,0:T(1,128)}, u32[]{:S(2)}, u32[]{:S(2)}) async-start(f32[32,1,3,2880]{3,1,2,0:T(1,128)} %copy.142), calls=%async_computation.4 | async-start | bytes 2260992 | tf_op jit(solution)/shard_map/all_to_all | solution.py:232
  252.6 106.5 %all-reduce.5.cloned.1.call-start = ((), (), s32[]{:S(2)}) async-start(), calls=%async_computation.6 | async-start | bytes 376832 | tf_op jit(solution)/shard_map/psum | solution.py:244
  (9 other events, 16.1 us)
Sparse Core Ops, SparseCore 0:
  139.9 65.6 all-reduce.2
  289.1 69.8 all-reduce.4
where the time goes:
time: 370 us; the launch traced here: 368 us
  waiting for transfers between devices  173 us (47%)
  local copies, waits for them, and re-layouts  57 us (15%)
  other arithmetic  36.6 us (10%)
  starting transfers between devices  35.4 us (10%)
  matrix products  26.8 us (7%)
  blocking collectives  25.1 us (7%)
  between operations  13.9 us (4%)
    psum x1, waiting for transfers between devices, on_device(): expert_total = lax.psum(expert_part, 'head')  70.1 us
    psum x1, waiting for transfers between devices, on_device(): projected = lax.psum(partial_proj, 'head')  65.8 us
    all_to_all x1, blocking collectives, on_device(): lax.all_to_all(outgoing, 'seq', split_axis=0, concat_axis=0, tiled=True)  25.1 us
    all_to_all x1, waiting for transfers between devices, on_device(): lax.all_to_all(jnp.einsum('nekf,efd->nekd', activation, down_weight, pref...  22.5 us
    all_to_all x1, starting transfers between devices, on_device(): lax.all_to_all(by_owner[1], 'seq', split_axis=0, concat_axis=0, tiled=True)  12.3 us
    unnamed x58, local copies, waits for them, and re-layouts  11.2 us
    dot_general x1, matrix products, on_device(): jnp.einsum('grtcjp,gpcd->grtcjd', prompt_weights.astype(jnp.bfloat16), pr...  9.51 us
    all_to_all x1, starting transfers between devices, on_device(): lax.all_to_all(by_owner[0], 'seq', split_axis=0, concat_axis=0, tiled=True)  9 us
  transfers between devices with their start and end apart: 6, of which 5 were waited for; matrix products, arithmetic and copies ran while one was open for 13% of the time, Pallas kernels for 0%

commit v1 on v0

v1 whole, which is shorter than its diff:
```python
import math

import jax
import jax.numpy as jnp
import numpy as np
from jax import lax
from jax.experimental import pallas as pl
from jax.experimental.pallas import tpu as pltpu
from jax.sharding import PartitionSpec as P

MESH = pl.DeviceIdType.MESH
LOW = -1e30
FLOOR = -1e29
F32 = jnp.float32
BF16 = jnp.bfloat16

N_SEQ = 32
N_HEAD = 8
REQ = 96
GROUPS = 8
MEMBERS = 12
PBLOCK = 1024
TBLOCK = 32
D = 2880
CH = 384
LASTC = 192
FFL = 360
ROWS = 96
NT = (((1,), (1,)), ((), ()))
NN = (((1,), (0,)), ((), ()))
TN = (((0,), (0,)), ((), ()))


def dot(a, b, dims):
    return lax.dot_general(a, b, dims, preferred_element_type=F32)


def iota(shape, axis):
    return lax.broadcasted_iota(jnp.int32, shape, axis)


def turned(x, cosine, sine, lane):
    ahead = pltpu.roll(x, 96, 1)
    behind = pltpu.roll(x, 32, 1)
    partner = jnp.where((lane & 63) < 32, -ahead, behind)
    return x * cosine + partner * sine


def tiles_of(out, peak, lane):
    first, second = out[:16], out[16:]
    values = jnp.where(lane < 64, pltpu.roll(first, 64, 1), second).astype(BF16)
    hi0 = first.astype(BF16).astype(F32)
    hi1 = second.astype(BF16).astype(F32)
    lo0 = first - hi0
    lo1 = second - hi1
    stats = jnp.where(
        lane < 4,
        jnp.where(lane == 0, peak[:16], jnp.where(lane == 1, hi0, jnp.where(lane == 2, lo0, 0.0))),
        jnp.where(
            lane == 4, peak[16:], jnp.where(lane == 5, hi1, jnp.where(lane == 6, lo1, 0.0))
        ),
    )
    return values, jnp.where(lane < 8, stats, 0.0)


def layer_kernel(
    order,
    rank,
    tail_lens,
    prompt_lens,
    sinks,
    cosb,
    sinb,
    steps_cos,
    steps_sin,
    fresh,
    ids,
    routes,
    resid,
    gain,
    q_hbm,
    prompt_hbm,
    tail_hbm,
    ow_hbm,
    gu_hbm,
    dn_hbm,
    out_ref,
    q_v,
    prompt_v,
    tail_v,
    ow_v,
    gu_v,
    dn_v,
    dn_last,
    q_all,
    acc_s,
    stat_s,
    msg1,
    rcv1,
    msg2,
    rcv2,
    msg3,
    rcv3,
    msg4,
    rcv4,
    msg5,
    rcv5,
    msg6,
    rcv6,
    msg7,
    rcv7,
    load_sem,
    prompt_sem,
    send1,
    recv1,
    send2,
    recv2,
    send3,
    recv3,
    send4,
    recv4,
    send5,
    recv5,
    send6,
    recv6,
    send7,
    recv7,
):
    me = lax.axis_index("seq")
    head = lax.axis_index("head")
    barrier = pltpu.get_barrier_semaphore()

    def greet_seq(d, carry):
        pl.semaphore_signal(
            barrier, inc=1, device_id=(lax.rem(me + d, N_SEQ), head), device_id_type=MESH
        )
        return carry

    def greet_head(d, carry):
        pl.semaphore_signal(
            barrier, inc=1, device_id=(me, lax.rem(head + d, N_HEAD)), device_id_type=MESH
        )
        return carry

    load_q = pltpu.make_async_copy(q_hbm, q_v, load_sem.at[0])
    load_tail = pltpu.make_async_copy(tail_hbm, tail_v, load_sem.at[1])
    load_ow = pltpu.make_async_copy(ow_hbm, ow_v.at[pl.ds(0, D)], load_sem.at[2])
    load_gu = pltpu.make_async_copy(gu_hbm, gu_v, load_sem.at[3])
    load_dn = pltpu.make_async_copy(dn_hbm, dn_v, load_sem.at[4])
    load_q.start()
    load_tail.start()

    def load_prompt(g):
        return pltpu.make_async_copy(prompt_hbm.at[g], prompt_v.at[g], prompt_sem.at[g])

    for g in range(GROUPS):
        load_prompt(g).start()
    load_ow.start()
    load_gu.start()
    load_dn.start()
    lax.fori_loop(1, N_SEQ, greet_seq, 0)
    lax.fori_loop(1, N_HEAD, greet_head, 0)

    lane = iota((16, 128), 1)
    row = iota((16, 128), 0)

    load_q.wait()
    ct = steps_cos[...]
    st = steps_sin[...]

    def rotate_one(i, carry):
        r = order[i]
        x = q_v[r].astype(F32)
        c0 = cosb[r]
        s0 = sinb[r]
        y = turned(x, c0 * ct - s0 * st, s0 * ct + c0 * st, lane)
        y = y.astype(BF16).astype(F32) * 0.125
        q_all[i, 0:16, :] = jnp.where(lane < 64, y, 0.0).astype(BF16)
        q_all[i, 16:32, :] = jnp.where(lane < 64, pltpu.roll(y, 64, 1), 0.0).astype(
            BF16
        )
        return carry

    lax.fori_loop(0, REQ, rotate_one, 0, unroll=4)
    load_tail.wait()

    pos_row = iota((1, PBLOCK), 1) + me * PBLOCK
    col128 = iota((1, 128), 1)
    big_lane = iota((PBLOCK, 128), 1)
    tail_lane = iota((128, 128), 1)
    same_req = (iota((128, 128), 0) >> 5) == (iota((128, 128), 1) >> 5)

    def one_group(g, carry):
        load_prompt(g).wait()
        kv = prompt_v[g]
        vx = jnp.where(big_lane < 64, jnp.ones_like(kv), kv)
        bias = jnp.where(pos_row < prompt_lens[g], 0.0, LOW)
        for b in range(3):
            base = g * MEMBERS + b * 4
            q = q_all[pl.ds(base, 4)].reshape(128, 128)
            members = [order[base + i] for i in range(4)]
            kt = jnp.concatenate([tail_v[r] for r in members], axis=0)
            vt = jnp.where(tail_lane < 64, jnp.ones_like(kt), kt)
            limit = jnp.zeros((1, 128), jnp.int32)
            for i in range(4):
                limit = jnp.where((col128 >> 5) == i, tail_lens[members[i]], limit)
            ok = ((col128 & 31) + me * TBLOCK) < limit
            tail_bias = jnp.where(ok, 0.0, LOW)
            s = dot(q, kv, NT) + bias
            s2 = jnp.where(same_req, dot(q, kt, NT) + tail_bias, LOW)
            peak = jnp.maximum(
                jnp.max(s, axis=1, keepdims=True), jnp.max(s2, axis=1, keepdims=True)
            )
            peak = jnp.maximum(peak, FLOOR).astype(BF16).astype(F32)
            w = jnp.exp(s - peak).astype(BF16)
            w2 = jnp.exp(s2 - peak).astype(BF16)
            o = dot(w, vx, NN) + dot(w2, vt, NN)
            for i in range(4):
                values, stats = tiles_of(
                    o[32 * i : 32 * i + 32], peak[32 * i : 32 * i + 32], lane
                )
                acc_s[base + i] = values
                stat_s[base + i] = stats
        return carry

    lax.fori_loop(0, GROUPS, one_group, 0)

    pl.semaphore_wait(barrier, N_SEQ - 1 + N_HEAD - 1)

    def pack(dst, slot, o):
        total = jnp.zeros((16, 128), F32)
        for i in range(3):
            k = rank[3 * o + i]
            dst[slot, 16 * i : 16 * i + 16, :] = acc_s[k]
            piece = stat_s[k]
            total = total + (piece if i == 0 else pltpu.roll(piece, 8 * i, 1))
        dst[slot, 48:64, :] = total.astype(BF16)

    def seq_copy(msg, rcv, send, recv, to):
        return pltpu.make_async_remote_copy(
            src_ref=msg.at[to],
            dst_ref=rcv.at[me],
            send_sem=send.at[to],
            recv_sem=recv.at[me],
            device_id=(to, head),
            device_id_type=MESH,
        )

    def seq_arrival(msg, rcv, send, recv, source):
        return pltpu.make_async_remote_copy(
            src_ref=msg.at[source],
            dst_ref=rcv.at[source],
            send_sem=send.at[source],
            recv_sem=recv.at[source],
            device_id=(source, head),
            device_id_type=MESH,
        )

    def head_copy(msg, slot, rcv, send, recv, to):
        return pltpu.make_async_remote_copy(
            src_ref=msg if slot is None else msg.at[slot],
            dst_ref=rcv.at[head],
            send_sem=send.at[to],
            recv_sem=recv.at[head],
            device_id=(me, to),
            device_id_type=MESH,
        )

    def head_arrival(msg, slot, rcv, send, recv, source):
        return pltpu.make_async_remote_copy(
            src_ref=msg if slot is None else msg.at[slot],
            dst_ref=rcv.at[source],
            send_sem=send.at[source],
            recv_sem=recv.at[source],
            device_id=(me, source),
            device_id_type=MESH,
        )

    def others(count, mine, body):
        def step(d, carry):
            body(lax.rem(mine + d, count))
            return carry

        lax.fori_loop(1, count, step, 0)

    def send_partials(o):
        pack(msg1, o, o)
        seq_copy(msg1, rcv1, send1, recv1, o).start()

    others(N_SEQ, me, send_partials)
    pack(rcv1, me, me)

    base_c = jnp.zeros((16, 128), F32)
    base_s = jnp.zeros((16, 128), F32)
    for i in range(3):
        base_c = jnp.where((row >> 2) == i, cosb[me * 3 + i], base_c)
        base_s = jnp.where((row >> 2) == i, sinb[me * 3 + i], base_s)
    kv_new = fresh[...].astype(F32)
    key_new = turned(kv_new, base_c * ct - base_s * st, base_s * ct + base_c * st, lane)
    kn = jnp.where(lane < 64, key_new, kv_new).astype(BF16)
    vn = jnp.where(lane < 64, 1.0, kv_new).astype(BF16)
    fresh_stats = jnp.zeros((16, 128), F32)
    srow = iota((32, 16), 0)
    scol = iota((32, 16), 1)
    for i in range(3):
        k = rank[3 * me + i]
        q = q_all[k]
        seen = ((scol >> 2) == i) & ((scol & 3) <= (srow & 3))
        s = jnp.where(seen, dot(q, kn, NT), LOW)
        peak = jnp.max(s, axis=1, keepdims=True).astype(BF16).astype(F32)
        w = jnp.exp(s - peak).astype(BF16)
        values, stats = tiles_of(dot(w, vn, NN), peak, lane)
        rcv1[N_SEQ, 16 * i : 16 * i + 16, :] = values
        fresh_stats = fresh_stats + (stats if i == 0 else pltpu.roll(stats, 8 * i, 1))
    rcv1[N_SEQ, 48:64, :] = fresh_stats.astype(BF16)

    sink = jnp.zeros((16, 128), F32)
    for j in range(8):
        here = ((row >> 2) == (j >> 1)) & ((lane >> 6) == (j & 1))
        sink = jnp.where(here, sinks[j], sink)

    wide_lane = iota((16, 512), 1)
    expert = wide_lane >> 4
    place = wide_lane & 15
    pick = (place >= 3).astype(jnp.int32) + (place >= 6).astype(jnp.int32)
    tile = place - 3 * pick
    named = jnp.zeros((16, 512), F32)
    share = jnp.zeros((16, 512), F32)
    for k in range(4):
        hit = ids[:, k : k + 1] == expert
        named = named + jnp.where(hit, 1.0, 0.0)
        share = share + jnp.where(hit, routes[:, k : k + 1], 0.0)
    below = (iota((16, 16), 1) < iota((16, 16), 0)).astype(F32).astype(BF16)
    earlier = dot(below, named.astype(BF16), NN)
    chosen = (named > 0.5) & (earlier == pick.astype(F32)) & (place < 9)
    chosen_tile = [chosen & (tile == c) for c in range(3)]
    select = jnp.concatenate([jnp.where(m, 1.0, 0.0) for m in chosen_tile], axis=0).astype(BF16)
    give = jnp.concatenate([jnp.where(m, share, 0.0) for m in chosen_tile], axis=0)
    give_hi = give.astype(BF16)
    give_lo = (give - give_hi.astype(F32)).astype(BF16)

    trow = iota((288, 512), 0)
    tcol = iota((288, 512), 1)
    ttile = (trow >= 96).astype(jnp.int32) + (trow >= 192).astype(jnp.int32)
    trest = trow - 96 * ttile
    spread = (
        ((trest & 31) == (tcol >> 4)) & ((tcol & 15) == 3 * (trest >> 5) + ttile)
    ).astype(F32).astype(BF16)

    load_ow.wait()
    ow_v[pl.ds(D, 3072 - D), :] = jnp.zeros((3072 - D, 512), BF16)
    load_gu.wait()
    load_dn.wait()
    dn_last[:, 0:LASTC] = dn_v[:, 7 * CH : 7 * CH + LASTC]
    dn_last[:, LASTC:CH] = jnp.zeros((FFL, CH - LASTC), BF16)

    others(N_SEQ, me, lambda s: seq_arrival(msg1, rcv1, send1, recv1, s).wait_recv())

    stat_rows = rcv1[:, 48:64, :].reshape((N_SEQ + 1) * 16, 128)
    er = iota((128, 384), 0)
    ec = iota((128, 384), 1)
    attended = []
    for i in range(3):
        spot = 8 * i + 4 * ((ec & 127) >> 6) + (ec >> 7)
        expand = (er == spot).astype(F32).astype(BF16)
        wide = dot(stat_rows, expand, NN)
        peaks = wide[:, 0:128].reshape(N_SEQ + 1, 16, 128)
        totals = (wide[:, 128:256] + wide[:, 256:384]).reshape(N_SEQ + 1, 16, 128)
        top = jnp.maximum(jnp.max(peaks, axis=0), sink)
        factor = jnp.exp(peaks - top[None])
        values = rcv1[:, 16 * i : 16 * i + 16, :].astype(F32)
        num = jnp.sum(values * factor, axis=0)
        den = jnp.sum(totals * factor, axis=0) + jnp.exp(sink - top)
        attended.append((num / den).astype(BF16))
    att = jnp.concatenate(attended, axis=0)
    rr = iota((64, 48), 0)
    rc = iota((64, 48), 1)
    want = ((rr & 15) >> 2) * 16 + (rr >> 4) * 4 + (rr & 3)
    regroup = (rc == want).astype(F32).astype(BF16)
    mixed = dot(regroup, att, NN).astype(BF16)
    flat = jnp.concatenate([mixed[16 * p : 16 * p + 16] for p in range(4)], axis=1)

    def project(j):
        rows = ow_v[pl.ds(pl.multiple_of(j * CH, CH), CH), :]
        return dot(flat, rows, NT).astype(BF16)

    def send_projection(j):
        msg2[j] = project(j)
        head_copy(msg2, j, rcv2, send2, recv2, j).start()

    others(N_HEAD, head, send_projection)
    rcv2[head] = project(head)
    others(N_HEAD, head, lambda s: head_arrival(msg2, s, rcv2, send2, recv2, s).wait_recv())
    total = resid[:, pl.ds(pl.multiple_of(head * CH, CH), CH)].astype(F32)
    total = total + jnp.sum(rcv2[...].astype(F32), axis=0)
    hidden = total.astype(BF16)
    hidden_rows = jnp.concatenate([hidden[:, 128 * c : 128 * c + 128] for c in range(3)], axis=0)

    msg3[...] = dot(select, hidden_rows, TN).astype(BF16).reshape(N_SEQ, 16, 128)
    others(N_SEQ, me, lambda o: seq_copy(msg3, rcv3, send3, recv3, o).start())
    rcv3[me] = msg3[me]
    others(N_SEQ, me, lambda s: seq_arrival(msg3, rcv3, send3, recv3, s).wait_recv())
    got = dot(spread, rcv3[...].reshape(512, 128), NN).astype(BF16)
    mine = jnp.concatenate([got[96 * c : 96 * c + 96] for c in range(3)], axis=1)
    msg4[...] = mine
    others(N_HEAD, head, lambda o: head_copy(msg4, None, rcv4, send4, recv4, o).start())
    rcv4[head] = mine

    gate = jnp.zeros((ROWS, FFL), F32)
    up = jnp.zeros((ROWS, FFL), F32)
    square = jnp.zeros((ROWS, 1), F32)
    for j in range(N_HEAD):

        @pl.when(head != j)
        def _():
            head_arrival(msg4, None, rcv4, send4, recv4, j).wait_recv()

        width = CH if j < N_HEAD - 1 else LASTC
        x = rcv4[j].astype(F32)
        square = square + jnp.sum(x * x, axis=1, keepdims=True)
        y = (x * gain[:, j * CH : j * CH + CH]).astype(BF16)[:, :width]
        gate = gate + dot(y, gu_v[0, :, j * CH : j * CH + width], NT)
        up = up + dot(y, gu_v[1, :, j * CH : j * CH + width], NT)
    scale = lax.rsqrt(square * (1.0 / D) + 1e-05)
    g = jnp.minimum(gate * scale, 7.0)
    u = jnp.clip(up * scale, -7.0, 7.0)
    active = ((u + 1.0) * g * jax.nn.sigmoid(1.702 * g)).astype(BF16)

    def send_expert(d, carry):
        j = lax.rem(head + d, N_HEAD)
        col = pl.multiple_of(jnp.minimum(j, N_HEAD - 2) * CH, CH)

        @pl.when(j < N_HEAD - 1)
        def _():
            msg5[j] = dot(active, dn_v[:, pl.ds(col, CH)], NN).astype(BF16)

        @pl.when(j == N_HEAD - 1)
        def _():
            msg5[j] = dot(active, dn_last[...], NN).astype(BF16)

        @pl.when(d < N_HEAD)
        def _():
            head_copy(msg5, j, rcv5, send5, recv5, j).start()

        return carry

    lax.fori_loop(1, N_HEAD + 1, send_expert, 0)
    rcv5[head] = msg5[head]
    others(N_HEAD, head, lambda s: head_arrival(msg5, s, rcv5, send5, recv5, s).wait_recv())
    summed = jnp.sum(rcv5[...].astype(F32), axis=0).astype(BF16)
    summed_rows = jnp.concatenate([summed[:, 128 * c : 128 * c + 128] for c in range(3)], axis=0)
    msg6[...] = dot(spread, summed_rows, TN).astype(BF16).reshape(N_SEQ, 16, 128)
    others(N_SEQ, me, lambda o: seq_copy(msg6, rcv6, send6, recv6, o).start())
    rcv6[me] = msg6[me]
    others(N_SEQ, me, lambda s: seq_arrival(msg6, rcv6, send6, recv6, s).wait_recv())
    back = rcv6[...].reshape(512, 128)
    added = dot(give_hi, back, NN) + dot(give_lo, back, NN)
    result = hidden_rows.astype(F32) + added
    result = jnp.concatenate([result[16 * c : 16 * c + 16] for c in range(3)], axis=1).astype(BF16)
    msg7[...] = result
    others(N_HEAD, head, lambda o: head_copy(msg7, None, rcv7, send7, recv7, o).start())
    rcv7[head] = result
    others(N_HEAD, head, lambda s: head_arrival(msg7, None, rcv7, send7, recv7, s).wait_recv())
    for j in range(N_HEAD):
        out_ref[:, j * CH : j * CH + CH] = rcv7[j]

    for msg, rcv, send, recv in (
        (msg1, rcv1, send1, recv1),
        (msg3, rcv3, send3, recv3),
        (msg6, rcv6, send6, recv6),
    ):
        others(N_SEQ, me, lambda o: seq_copy(msg, rcv, send, recv, o).wait_send())
    for msg, whole, rcv, send, recv in (
        (msg2, False, rcv2, send2, recv2),
        (msg4, True, rcv4, send4, recv4),
        (msg5, False, rcv5, send5, recv5),
        (msg7, True, rcv7, send7, recv7),
    ):
        others(
            N_HEAD,
            head,
            lambda o: head_copy(msg, None if whole else o, rcv, send, recv, o).wait_send(),
        )


def on_device(
    new_query,
    fresh_key_value,
    prompt_cache,
    decoded_tail_cache,
    sinks,
    prompt_group,
    prompt_lens,
    tail_lens,
    o_weight,
    resid,
    norm_gain,
    expert_ids,
    route_weights,
    gate_up,
    down_weight,
):
    me = lax.axis_index("seq")
    r = jnp.arange(REQ, dtype=jnp.int32)
    code = prompt_group * REQ + r
    rank = jnp.sum((code[None, :] < code[:, None]).astype(jnp.int32), axis=1)
    order = jnp.sum(jnp.where(rank[None, :] == r[:, None], r[None, :], 0), axis=1)
    hot = prompt_group[:, None] == jnp.arange(GROUPS, dtype=jnp.int32)[None, :]
    start = jnp.sum(jnp.where(hot, prompt_lens[None, :], 0), axis=1)
    base = (start + tail_lens).astype(F32)
    frequency = jnp.exp(jnp.arange(32, dtype=F32) * (-2.0 * math.log(150000.0) / 64))
    angle = base[:, None] * jnp.tile(frequency, 4)[None, :]
    cosb, sinb = jnp.cos(angle)[:, None, :], jnp.sin(angle)[:, None, :]
    freq = np.exp(np.arange(32) * (-2.0 * math.log(150000.0) / 64))
    step_angle = (np.arange(16) % 4)[:, None] * np.tile(freq, 4)[None, :]
    steps_cos = jnp.asarray(np.cos(step_angle), F32)
    steps_sin = jnp.asarray(np.sin(step_angle), F32)
    fresh = jnp.pad(fresh_key_value.reshape(12, 128), ((0, 4), (0, 0)))
    own_ids = lax.dynamic_slice_in_dim(expert_ids, me * 3, 3, 0).reshape(12, 4)
    own_ids = jnp.pad(own_ids, ((0, 4), (0, 0)), constant_values=-1)
    routes = jnp.pad(route_weights.reshape(12, 4), ((0, 4), (0, 0)))
    resid16 = jnp.pad(resid.reshape(12, D), ((0, 4), (0, 3072 - D)))
    gain = jnp.pad(norm_gain, (0, 3072 - D)).reshape(1, 3072)
    q = new_query.reshape(REQ, 4, 4, 128).transpose(0, 2, 1, 3).reshape(REQ, 16, 128)
    prompt = prompt_cache.transpose(0, 2, 1, 3).reshape(GROUPS, PBLOCK, 128)
    tail = decoded_tail_cache.transpose(0, 2, 1, 3).reshape(REQ, TBLOCK, 128)
    ow = o_weight.T
    gu = gate_up.transpose(0, 2, 3, 1).reshape(2, FFL, D)
    dn = down_weight.reshape(FFL, D)

    smem = pl.BlockSpec(memory_space=pltpu.SMEM)
    vmem = pl.BlockSpec(memory_space=pltpu.VMEM)
    hbm = pl.BlockSpec(memory_space=pl.ANY)
    seq_sem = pltpu.SemaphoreType.DMA((N_SEQ,))
    head_sem = pltpu.SemaphoreType.DMA((N_HEAD,))
    out = pl.pallas_call(
        layer_kernel,
        name="layer",
        out_shape=jax.ShapeDtypeStruct((16, 3072), BF16),
        in_specs=[smem] * 5 + [vmem] * 9 + [hbm] * 6,
        out_specs=vmem,
        scratch_shapes=[
            pltpu.VMEM((REQ, 16, 128), BF16),
            pltpu.VMEM((GROUPS, PBLOCK, 128), BF16),
            pltpu.VMEM((REQ, TBLOCK, 128), BF16),
            pltpu.VMEM((3072, 512), BF16),
            pltpu.VMEM((2, FFL, D), BF16),
            pltpu.VMEM((FFL, D), BF16),
            pltpu.VMEM((FFL, CH), BF16),
            pltpu.VMEM((REQ, 32, 128), BF16),
            pltpu.VMEM((REQ, 16, 128), BF16),
            pltpu.VMEM((REQ, 16, 128), F32),
            pltpu.VMEM((N_SEQ, 64, 128), BF16),
            pltpu.VMEM((N_SEQ + 1, 64, 128), BF16),
            pltpu.VMEM((N_HEAD, 16, CH), BF16),
            pltpu.VMEM((N_HEAD, 16, CH), BF16),
            pltpu.VMEM((N_SEQ, 16, 128), BF16),
            pltpu.VMEM((N_SEQ, 16, 128), BF16),
            pltpu.VMEM((ROWS, CH), BF16),
            pltpu.VMEM((N_HEAD, ROWS, CH), BF16),
            pltpu.VMEM((N_HEAD, ROWS, CH), BF16),
            pltpu.VMEM((N_HEAD, ROWS, CH), BF16),
            pltpu.VMEM((N_SEQ, 16, 128), BF16),
            pltpu.VMEM((N_SEQ, 16, 128), BF16),
            pltpu.VMEM((16, CH), BF16),
            pltpu.VMEM((N_HEAD, 16, CH), BF16),
            pltpu.SemaphoreType.DMA((5,)),
            pltpu.SemaphoreType.DMA((GROUPS,)),
            seq_sem,
            seq_sem,
            head_sem,
            head_sem,
            seq_sem,
            seq_sem,
            head_sem,
            head_sem,
            head_sem,
            head_sem,
            seq_sem,
            seq_sem,
            head_sem,
            head_sem,
        ],
        compiler_params=pltpu.CompilerParams(
            collective_id=0, has_side_effects=True, vmem_limit_bytes=56 * 1024 * 1024
        ),
    )(
        order,
        rank,
        tail_lens,
        prompt_lens,
        sinks,
        cosb,
        sinb,
        steps_cos,
        steps_sin,
        fresh,
        own_ids,
        routes,
        resid16,
        gain,
        q,
        prompt,
        tail,
        ow,
        gu,
        dn,
    )
    return out[:12, :D].reshape(3, 4, D)


def solution(mesh):
    return jax.shard_map(
        on_device,
        mesh=mesh,
        in_specs=(
            P(None, None, "head"),
            P("seq", None, "head", None),
            P(None, "seq", "head", None),
            P(None, "seq", "head", None),
            P("head"),
            P(),
            P(),
            P(),
            P("head", None),
            P("seq", None, None),
            P(),
            P(),
            P("seq", None, None),
            P("seq", None, None, "head"),
            P("seq", "head", None),
        ),
        out_specs=P("seq", None, None),
        check_vma=False,
    )
```

time: 370 us -> 100 us (0.27)
  waiting for transfers between devices: 173 us -> 0 us
  Pallas kernels: 0 us -> 86.7 us
  local copies, waits for them, and re-layouts: 57 us -> 8.03 us
  starting transfers between devices: 35.4 us -> 0 us
  other arithmetic: 36.6 us -> 4.99 us
  matrix products: 26.8 us -> 0 us
  blocking collectives: 25.1 us -> 0 us
  between operations: 13.9 us -> 0.04 us
    psum x2 -> x0, waiting for transfers between devices: 136 us -> none  [the longest x1 70.1 us: on_device(): expert_total = lax.psum(expert_part, 'head')]
    pallas_call x0 -> x1, Pallas kernels: none -> 86.7 us  [on_device(): pl.pallas_call(layer_kernel, name='layer', out_shape=jax.ShapeDtypeStruct...]
    all_to_all x4 -> x0, waiting for transfers between devices: 36.8 us -> none  [the longest x1 22.5 us: on_device(): lax.all_to_all(jnp.einsum('nekf,efd->nekd', activation, down_weight, pref...]
    all_to_all x4 -> x0, starting transfers between devices: 34.8 us -> none  [the longest x1 12.3 us: on_device(): lax.all_to_all(by_owner[1], 'seq', split_axis=0, concat_axis=0, tiled=True)]
    dot_general x9 -> x0, matrix products: 26.8 us -> none  [the longest x1 9.51 us: on_device(): jnp.einsum('grtcjp,gpcd->grtcjd', prompt_weights.astype(jnp.bfloat16), pr...]
    all_to_all x1 -> x0, blocking collectives: 25.1 us -> none  [on_device(): lax.all_to_all(outgoing, 'seq', split_axis=0, concat_axis=0, tiled=True)]
    reshape x14 -> x6, local copies, waits for them, and re-layouts: 20.3 us -> 3.14 us  [the longest x1 0.93 us: on_device(): resid16 = jnp.pad(resid.reshape(12, D), ((0, 4), (0, 3072 - D)))]
    gather x6 -> x0, local copies, waits for them, and re-layouts: 11.7 us -> none  [the longest x1 3.17 us: on_device(): prompt_acc.reshape(requests, steps_total, query_width)[inverse]]
  transfers between devices with their start and end apart: 6 -> 0, of which waited for: 5 -> 0; matrix products, arithmetic and copies ran while one was open for 13% -> 0% of each run, Pallas kernels for 0% -> 0%
where the time goes in v1:
time: 100 us; the launch traced here: 99.8 us
  Pallas kernels  86.7 us (87%)
  local copies, waits for them, and re-layouts  8.03 us (8%)
  other arithmetic  4.99 us (5%)
    pallas_call x1, Pallas kernels, on_device(): pl.pallas_call(layer_kernel, name='layer', out_shape=jax.ShapeDtypeStruct...  86.7 us
    sin x1, other arithmetic, on_device(): cosb, sinb = (jnp.cos(angle)[:, None, :], jnp.sin(angle)[:, None, :])  2.02 us

profile of v1, /device:TPU:1, one launch (start us, length us, event | category | flops | bytes accessed | tf_op | source)
XLA Modules:
  0.0 99.8 jit_solution(7958331877742172749)
XLA Ops:
  0.0 0.0 copy-start
  0.0 0.8 select_reduce_fusion.1
  0.8 0.7 add_convert_fusion
  1.4 0.7 iota_add_fusion
  2.1 0.2 convert_reduce_fusion.rank
  2.3 0.0 copy-start.1
  2.3 0.7 select_reduce_fusion.order
  3.0 0.1 mul.50
  3.1 0.7 reshape.140
  3.8 0.6 pad.20.fresh
  4.4 0.0 copy-done
  4.4 0.1 constant_dynamic-slice_fusion
  4.5 0.1 copy.39
  4.6 0.6 pad.21.ids
  5.2 0.7 reshape.151
  5.9 0.6 pad.22.routes
  6.5 1.3 %pad.24 = f32[3072]{0:T(1024)} pad(f32[2880]{0:T(1024)} %param.27, f32[]{:T(128)} %constant.24.clone.1), padding=0_192 | pad | bytes 23812 | tf_op jit(solution)/shard_map/jit(_pad)/pad | solution.py:523
  7.8 0.1 mul.47
  7.9 2.0 %multiply_sine_fusion = (f32[96,1,128]{2,1,0:T(1,128)}, f32[96,1,128]{2,1,0:T(1,128)}) fusion(f32[96,1,128]{2,1,0:T(1,128)S(1)} %bitcast.22, f32[128]{0:T(128)S(1)} %mul.50), kind=kLoop, calls=%fused_computation.3 | loop fusion | flops 12288 | bytes 147968 | tf_op jit(solution)/shard_map/sin | solution.py:513
  9.9 0.9 reshape.143
  10.8 0.6 pad.23.resid
  11.5 86.7 %layer.1 = bf16[16,3072]{1,0:T(8,128)(2,1)} custom-call(s32[96]{0:T(128)} %select_reduce_fusion.order, s32[96]{0:T(128)} %copy-done.1, s32[96]{0:T(128)} %tail_lens.1, s32[8]{0:T(128)} %prompt_lens.1, f32[8]{0:T(128)} %sinks.1, f32[96,1,128]{2,1,0:T(1,128)} %get-tuple-element.6.cosb, f32[96,1,128]{2,1,0:T(1,128)} %get-tuple-element.5.sinb, ...), custom_call_target="tpu_custom_call" | custom-call | tf_op jit(solution)/shard_map/layer/pallas_call | solution.py:536
  98.2 0.9 slice.3
  99.1 0.7 reshape.149
  (4 shorter events, 0.0 us)
Async XLA Ops:
  0.0 4.4 %copy-start = (s32[96,4,4]{0,2,1:T(4,128)S(1)}, s32[96,4,4]{0,2,1:T(4,128)}, u32[]{:S(2)}) copy-start(s32[96,4,4]{0,2,1:T(4,128)} %param.28) | copy-start | bytes 18436
  2.3 9.2 %copy-start.1 = (s32[96]{0:T(128)}, s32[96]{0:T(128)S(1)}, u32[]{:S(2)}) copy-start(s32[96]{0:T(128)S(1)} %convert_reduce_fusion.rank) | copy-start | bytes 1156

commit v2 on v1

--- a/solution.py
+++ b/solution.py
@@ -26,6 +26,7 @@
 LASTC = 192
 FFL = 360
 ROWS = 96
+HALF_PI = (1.5703125, 4.8351287841796875e-4, 3.1391647865048e-7)
 NT = (((1,), (1,)), ((), ()))
 NN = (((1,), (0,)), ((), ()))
 TN = (((0,), (0,)), ((), ()))
@@ -44,6 +45,23 @@
     behind = pltpu.roll(x, 32, 1)
     partner = jnp.where((lane & 63) < 32, -ahead, behind)
     return x * cosine + partner * sine
+
+
+def cos_sin(angle):
+    k = jnp.floor(angle * (2.0 / math.pi) + 0.5)
+    r = angle - k * HALF_PI[0]
+    r = r - k * HALF_PI[1]
+    r = r - k * HALF_PI[2]
+    r2 = r * r
+    s = r + r * r2 * (-1.0 / 6 + r2 * (1.0 / 120 + r2 * (-1.0 / 5040 + r2 * (1.0 / 362880))))
+    c = 1.0 + r2 * (-0.5 + r2 * (1.0 / 24 + r2 * (-1.0 / 720 + r2 * (1.0 / 40320))))
+    quarter = k - 4.0 * jnp.floor(k * 0.25)
+    odd = (quarter == 1.0) | (quarter == 3.0)
+    cosine = jnp.where(odd, s, c)
+    sine = jnp.where(odd, c, s)
+    cosine = jnp.where((quarter == 1.0) | (quarter == 2.0), -cosine, cosine)
+    sine = jnp.where(quarter >= 2.0, -sine, sine)
+    return cosine, sine
 
 
 def tiles_of(out, peak, lane):
@@ -66,13 +84,11 @@
 def layer_kernel(
     order,
     rank,
+    prompt_group,
     tail_lens,
     prompt_lens,
     sinks,
-    cosb,
-    sinb,
-    steps_cos,
-    steps_sin,
+    tables,
     fresh,
     ids,
     routes,
@@ -92,6 +108,11 @@
     gu_v,
     dn_v,
     dn_last,
+    cos_s,
+    sin_s,
+    small_s,
+    route_s,
+    resid_s,
     q_all,
     acc_s,
     stat_s,
@@ -145,8 +166,9 @@
     load_q = pltpu.make_async_copy(q_hbm, q_v, load_sem.at[0])
     load_tail = pltpu.make_async_copy(tail_hbm, tail_v, load_sem.at[1])
     load_ow = pltpu.make_async_copy(ow_hbm, ow_v.at[pl.ds(0, D)], load_sem.at[2])
-    load_gu = pltpu.make_async_copy(gu_hbm, gu_v, load_sem.at[3])
-    load_dn = pltpu.make_async_copy(dn_hbm, dn_v, load_sem.at[4])
+    load_gate = pltpu.make_async_copy(gu_hbm.at[0], gu_v.at[pl.ds(0, FFL)], load_sem.at[3])
+    load_up = pltpu.make_async_copy(gu_hbm.at[1], gu_v.at[pl.ds(CH, FFL)], load_sem.at[5])
+    load_dn = pltpu.make_async_copy(dn_hbm, dn_v.at[pl.ds(0, FFL)], load_sem.at[4])
     load_q.start()
     load_tail.start()
 
@@ -156,7 +178,8 @@
     for g in range(GROUPS):
         load_prompt(g).start()
     load_ow.start()
-    load_gu.start()
+    load_gate.start()
+    load_up.start()
     load_dn.start()
     lax.fori_loop(1, N_SEQ, greet_seq, 0)
     lax.fori_loop(1, N_HEAD, greet_head, 0)
@@ -164,63 +187,84 @@
     lane = iota((16, 128), 1)
     row = iota((16, 128), 0)
 
+    freq = tables[0:1, :]
+    ct = tables[8:24, :]
+    st = tables[24:40, :]
+
+    def place(r):
+        return (prompt_lens[prompt_group[r]] + tail_lens[r]).astype(F32)
+
+    def put_angle(i, carry):
+        cos_s[pl.ds(i, 1), :] = freq * place(order[i])
+        return carry
+
+    lax.fori_loop(0, REQ, put_angle, 0, unroll=8)
+    cosine, sine = cos_sin(cos_s[...])
+    cos_s[...] = cosine
+    sin_s[...] = sine
+
     load_q.wait()
-    ct = steps_cos[...]
-    st = steps_sin[...]
+
+    unit = jnp.where(lane == 64, 1.0, 0.0)
 
     def rotate_one(i, carry):
         r = order[i]
         x = q_v[r].astype(F32)
-        c0 = cosb[r]
-        s0 = sinb[r]
+        c0 = cos_s[pl.ds(i, 1), :]
+        s0 = sin_s[pl.ds(i, 1), :]
         y = turned(x, c0 * ct - s0 * st, s0 * ct + c0 * st, lane)
         y = y.astype(BF16).astype(F32) * 0.125
-        q_all[i, 0:16, :] = jnp.where(lane < 64, y, 0.0).astype(BF16)
-        q_all[i, 16:32, :] = jnp.where(lane < 64, pltpu.roll(y, 64, 1), 0.0).astype(
-            BF16
-        )
+        q_all[i, 0:16, :] = jnp.where(lane < 64, y, unit).astype(BF16)
+        q_all[i, 16:32, :] = jnp.where(
+            lane < 64, pltpu.roll(y, 64, 1), unit
+        ).astype(BF16)
         return carry
 
     lax.fori_loop(0, REQ, rotate_one, 0, unroll=4)
     load_tail.wait()
 
-    pos_row = iota((1, PBLOCK), 1) + me * PBLOCK
+    key_row = iota((PBLOCK, 128), 0) + me * PBLOCK
+    key_lane = iota((PBLOCK, 128), 1)
     col128 = iota((1, 128), 1)
-    big_lane = iota((PBLOCK, 128), 1)
     tail_lane = iota((128, 128), 1)
     same_req = (iota((128, 128), 0) >> 5) == (iota((128, 128), 1) >> 5)
 
     def one_group(g, carry):
         load_prompt(g).wait()
+        first = g * MEMBERS
         kv = prompt_v[g]
-        vx = jnp.where(big_lane < 64, jnp.ones_like(kv), kv)
-        bias = jnp.where(pos_row < prompt_lens[g], 0.0, LOW)
+        bias = jnp.where(key_row < prompt_lens[g], 0.0, LOW).astype(BF16)
+        kx = jnp.where(key_lane < 64, kv, bias)
+        vx = jnp.where(key_lane < 64, jnp.ones_like(kv), kv)
+        q = q_all[pl.ds(first, MEMBERS)].reshape(MEMBERS * 32, 128)
+        s = dot(q, kx, NT)
+        members = [order[first + i] for i in range(MEMBERS)]
+        s2 = []
+        vt = []
         for b in range(3):
-            base = g * MEMBERS + b * 4
-            q = q_all[pl.ds(base, 4)].reshape(128, 128)
-            members = [order[base + i] for i in range(4)]
-            kt = jnp.concatenate([tail_v[r] for r in members], axis=0)
-            vt = jnp.where(tail_lane < 64, jnp.ones_like(kt), kt)
+            kt = jnp.concatenate([tail_v[r] for r in members[4 * b : 4 * b + 4]], axis=0)
             limit = jnp.zeros((1, 128), jnp.int32)
             for i in range(4):
-                limit = jnp.where((col128 >> 5) == i, tail_lens[members[i]], limit)
-            ok = ((col128 & 31) + me * TBLOCK) < limit
-            tail_bias = jnp.where(ok, 0.0, LOW)
-            s = dot(q, kv, NT) + bias
-            s2 = jnp.where(same_req, dot(q, kt, NT) + tail_bias, LOW)
-            peak = jnp.maximum(
-                jnp.max(s, axis=1, keepdims=True), jnp.max(s2, axis=1, keepdims=True)
-            )
-            peak = jnp.maximum(peak, FLOOR).astype(BF16).astype(F32)
-            w = jnp.exp(s - peak).astype(BF16)
-            w2 = jnp.exp(s2 - peak).astype(BF16)
-            o = dot(w, vx, NN) + dot(w2, vt, NN)
+                limit = jnp.where((col128 >> 5) == i, tail_lens[members[4 * b + i]], limit)
+            seen = same_req & (((col128 & 31) + me * TBLOCK) < limit)
+            qt = jnp.where(tail_lane < 64, q[128 * b : 128 * b + 128], jnp.zeros_like(kt))
+            s2.append(jnp.where(seen, dot(qt, kt, NT), LOW))
+            vt.append(jnp.where(tail_lane < 64, jnp.ones_like(kt), kt))
+        s2 = jnp.concatenate(s2, axis=0)
+        peak = jnp.maximum(jnp.max(s, axis=1, keepdims=True), jnp.max(s2, axis=1, keepdims=True))
+        peak = jnp.maximum(peak, FLOOR).astype(BF16).astype(F32)
+        w = jnp.exp(s - peak).astype(BF16)
+        w2 = jnp.exp(s2 - peak).astype(BF16)
+        o = dot(w, vx, NN)
+        for b in range(3):
+            ob = o[128 * b : 128 * b + 128] + dot(w2[128 * b : 128 * b + 128], vt[b], NN)
+            pb = peak[128 * b : 128 * b + 128]
             for i in range(4):
                 values, stats = tiles_of(
-                    o[32 * i : 32 * i + 32], peak[32 * i : 32 * i + 32], lane
+                    ob[32 * i : 32 * i + 32], pb[32 * i : 32 * i + 32], lane
                 )
-                acc_s[base + i] = values
-                stat_s[base + i] = stats
+                acc_s[first + 4 * b + i] = values
+                stat_s[first + 4 * b + i] = stats
         return carry
 
     lax.fori_loop(0, GROUPS, one_group, 0)
@@ -290,12 +334,13 @@
     others(N_SEQ, me, send_partials)
     pack(rcv1, me, me)
 
-    base_c = jnp.zeros((16, 128), F32)
-    base_s = jnp.zeros((16, 128), F32)
+    angle = jnp.zeros((16, 128), F32)
     for i in range(3):
-        base_c = jnp.where((row >> 2) == i, cosb[me * 3 + i], base_c)
-        base_s = jnp.where((row >> 2) == i, sinb[me * 3 + i], base_s)
-    kv_new = fresh[...].astype(F32)
+        angle = jnp.where((row >> 2) == i, freq * place(me * 3 + i), angle)
+        small_s[4 * i : 4 * i + 4, :] = fresh[i].astype(F32)
+    base_c, base_s = cos_sin(angle)
+    small_s[12:16, :] = jnp.zeros((4, 128), F32)
+    kv_new = small_s[...]
     key_new = turned(kv_new, base_c * ct - base_s * st, base_s * ct + base_c * st, lane)
     kn = jnp.where(lane < 64, key_new, kv_new).astype(BF16)
     vn = jnp.where(lane < 64, 1.0, kv_new).astype(BF16)
@@ -306,6 +351,7 @@
         k = rank[3 * me + i]
         q = q_all[k]
         seen = ((scol >> 2) == i) & ((scol & 3) <= (srow & 3))
+        q = jnp.where(iota((32, 128), 1) < 64, q, jnp.zeros_like(q))
         s = jnp.where(seen, dot(q, kn, NT), LOW)
         peak = jnp.max(s, axis=1, keepdims=True).astype(BF16).astype(F32)
         w = jnp.exp(s - peak).astype(BF16)
@@ -324,17 +370,33 @@
     place = wide_lane & 15
     pick = (place >= 3).astype(jnp.int32) + (place >= 6).astype(jnp.int32)
     tile = place - 3 * pick
+    own = (iota((REQ, 384), 0) == me * 3 + (iota((REQ, 384), 1) >> 7)).astype(F32).astype(BF16)
+    flat_ids = jnp.concatenate([ids[t] for t in range(4)], axis=0).astype(F32).astype(BF16)
+    own_ids = dot(flat_ids, own, NN).astype(BF16)
+    xr = iota((64, 16), 0)
+    xc = iota((64, 16), 1)
+    names = jnp.full((64, 128), -1.0, F32) * ((iota((64, 128), 0) & 15) >= 12).astype(F32)
+    for i in range(3):
+        take = (xc == (xr & 3) * 4 + (xr >> 4)) & (((xr & 15) >> 2) == i)
+        names = names + dot(
+            take.astype(F32).astype(BF16), own_ids[:, 128 * i : 128 * i + 128], NN
+        )
+    names = jnp.concatenate([names] * 4, axis=1)
+    route_s[...] = jnp.zeros((16, 128), F32)
+    for i in range(3):
+        route_s[4 * i : 4 * i + 4, 0:4] = routes[i]
     named = jnp.zeros((16, 512), F32)
     share = jnp.zeros((16, 512), F32)
     for k in range(4):
-        hit = ids[:, k : k + 1] == expert
+        hit = names[16 * k : 16 * k + 16] == expert.astype(F32)
         named = named + jnp.where(hit, 1.0, 0.0)
-        share = share + jnp.where(hit, routes[:, k : k + 1], 0.0)
+        share = share + jnp.where(hit, route_s[:, k : k + 1], 0.0)
     below = (iota((16, 16), 1) < iota((16, 16), 0)).astype(F32).astype(BF16)
     earlier = dot(below, named.astype(BF16), NN)
     chosen = (named > 0.5) & (earlier == pick.astype(F32)) & (place < 9)
     chosen_tile = [chosen & (tile == c) for c in range(3)]
-    select = jnp.concatenate([jnp.where(m, 1.0, 0.0) for m in chosen_tile], axis=0).astype(BF16)
+    select = jnp.concatenate([jnp.where(m, 1.0, 0.0) for m in chosen_tile], axis=0)
+    select = select.T.astype(BF16)
     give = jnp.concatenate([jnp.where(m, share, 0.0) for m in chosen_tile], axis=0)
     give_hi = give.astype(BF16)
     give_lo = (give - give_hi.astype(F32)).astype(BF16)
@@ -347,12 +409,27 @@
         ((trest & 31) == (tcol >> 4)) & ((tcol & 15) == 3 * (trest >> 5) + ttile)
     ).astype(F32).astype(BF16)
 
+    ucol = iota((512, 288), 1)
+    urow = iota((512, 288), 0)
+    utile = (ucol >= 96).astype(jnp.int32) + (ucol >= 192).astype(jnp.int32)
+    urest = ucol - 96 * utile
+    gather = (
+        ((urest & 31) == (urow >> 4)) & ((urow & 15) == 3 * (urest >> 5) + utile)
+    ).astype(F32).astype(BF16)
+    resid_s[...] = jnp.zeros((16, 3072), F32)
+    for i in range(3):
+        resid_s[4 * i : 4 * i + 4, 0:D] = resid[i].astype(F32)
+
     load_ow.wait()
     ow_v[pl.ds(D, 3072 - D), :] = jnp.zeros((3072 - D, 512), BF16)
-    load_gu.wait()
+    load_gate.wait()
+    load_up.wait()
     load_dn.wait()
+    gu_v[FFL:CH, :] = jnp.zeros((CH - FFL, D), BF16)
+    gu_v[CH + FFL : 2 * CH, :] = jnp.zeros((CH - FFL, D), BF16)
+    dn_v[FFL:CH, :] = jnp.zeros((CH - FFL, D), BF16)
     dn_last[:, 0:LASTC] = dn_v[:, 7 * CH : 7 * CH + LASTC]
-    dn_last[:, LASTC:CH] = jnp.zeros((FFL, CH - LASTC), BF16)
+    dn_last[:, LASTC:CH] = jnp.zeros((CH, CH - LASTC), BF16)
 
     others(N_SEQ, me, lambda s: seq_arrival(msg1, rcv1, send1, recv1, s).wait_recv())
 
@@ -391,12 +468,12 @@
     others(N_HEAD, head, send_projection)
     rcv2[head] = project(head)
     others(N_HEAD, head, lambda s: head_arrival(msg2, s, rcv2, send2, recv2, s).wait_recv())
-    total = resid[:, pl.ds(pl.multiple_of(head * CH, CH), CH)].astype(F32)
+    total = resid_s[:, pl.ds(pl.multiple_of(head * CH, CH), CH)]
     total = total + jnp.sum(rcv2[...].astype(F32), axis=0)
     hidden = total.astype(BF16)
     hidden_rows = jnp.concatenate([hidden[:, 128 * c : 128 * c + 128] for c in range(3)], axis=0)
 
-    msg3[...] = dot(select, hidden_rows, TN).astype(BF16).reshape(N_SEQ, 16, 128)
+    msg3[...] = dot(select, hidden_rows, NN).astype(BF16).reshape(N_SEQ, 16, 128)
     others(N_SEQ, me, lambda o: seq_copy(msg3, rcv3, send3, recv3, o).start())
     rcv3[me] = msg3[me]
     others(N_SEQ, me, lambda s: seq_arrival(msg3, rcv3, send3, recv3, s).wait_recv())
@@ -406,24 +483,25 @@
     others(N_HEAD, head, lambda o: head_copy(msg4, None, rcv4, send4, recv4, o).start())
     rcv4[head] = mine
 
-    gate = jnp.zeros((ROWS, FFL), F32)
-    up = jnp.zeros((ROWS, FFL), F32)
+    both = jnp.zeros((ROWS, 2 * CH), F32)
     square = jnp.zeros((ROWS, 1), F32)
-    for j in range(N_HEAD):
-
-        @pl.when(head != j)
-        def _():
-            head_arrival(msg4, None, rcv4, send4, recv4, j).wait_recv()
-
-        width = CH if j < N_HEAD - 1 else LASTC
-        x = rcv4[j].astype(F32)
-        square = square + jnp.sum(x * x, axis=1, keepdims=True)
-        y = (x * gain[:, j * CH : j * CH + CH]).astype(BF16)[:, :width]
-        gate = gate + dot(y, gu_v[0, :, j * CH : j * CH + width], NT)
-        up = up + dot(y, gu_v[1, :, j * CH : j * CH + width], NT)
+    for half in range(2):
+        parts = []
+        for j in range(4 * half, 4 * half + 4):
+
+            @pl.when(head != j)
+            def _():
+                head_arrival(msg4, None, rcv4, send4, recv4, j).wait_recv()
+
+            width = CH if j < N_HEAD - 1 else LASTC
+            x = rcv4[j, :, 0:width].astype(F32)
+            square = square + jnp.sum(x * x, axis=1, keepdims=True)
+            parts.append((x * gain[:, j * CH : j * CH + width]).astype(BF16))
+        stop = min(D, 4 * (half + 1) * CH)
+        both = both + dot(jnp.concatenate(parts, axis=1), gu_v[:, 4 * half * CH : stop], NT)
     scale = lax.rsqrt(square * (1.0 / D) + 1e-05)
-    g = jnp.minimum(gate * scale, 7.0)
-    u = jnp.clip(up * scale, -7.0, 7.0)
+    g = jnp.minimum(both[:, 0:CH] * scale, 7.0)
+    u = jnp.clip(both[:, CH : 2 * CH] * scale, -7.0, 7.0)
     active = ((u + 1.0) * g * jax.nn.sigmoid(1.702 * g)).astype(BF16)
 
     def send_expert(d, carry):
@@ -449,7 +527,7 @@
     others(N_HEAD, head, lambda s: head_arrival(msg5, s, rcv5, send5, recv5, s).wait_recv())
     summed = jnp.sum(rcv5[...].astype(F32), axis=0).astype(BF16)
     summed_rows = jnp.concatenate([summed[:, 128 * c : 128 * c + 128] for c in range(3)], axis=0)
-    msg6[...] = dot(spread, summed_rows, TN).astype(BF16).reshape(N_SEQ, 16, 128)
+    msg6[...] = dot(gather, summed_rows, NN).astype(BF16).reshape(N_SEQ, 16, 128)
     others(N_SEQ, me, lambda o: seq_copy(msg6, rcv6, send6, recv6, o).start())
     rcv6[me] = msg6[me]
     others(N_SEQ, me, lambda s: seq_arrival(msg6, rcv6, send6, recv6, s).wait_recv())
@@ -461,8 +539,10 @@
     others(N_HEAD, head, lambda o: head_copy(msg7, None, rcv7, send7, recv7, o).start())
     rcv7[head] = result
     others(N_HEAD, head, lambda s: head_arrival(msg7, None, rcv7, send7, recv7, s).wait_recv())
-    for j in range(N_HEAD):
-        out_ref[:, j * CH : j * CH + CH] = rcv7[j]
+    for i in range(3):
+        for j in range(N_HEAD):
+            width = CH if j < N_HEAD - 1 else LASTC
+            out_ref[i, :, j * CH : j * CH + width] = rcv7[j, 4 * i : 4 * i + 4, 0:width]
 
     for msg, rcv, send, recv in (
         (msg1, rcv1, send1, recv1),
@@ -500,27 +580,21 @@
     gate_up,
     down_weight,
 ):
-    me = lax.axis_index("seq")
     r = jnp.arange(REQ, dtype=jnp.int32)
-    code = prompt_group * REQ + r
-    rank = jnp.sum((code[None, :] < code[:, None]).astype(jnp.int32), axis=1)
+    mine, other = prompt_group[:, None], prompt_group[None, :]
+    ahead = (other < mine) | ((other == mine) & (r[None, :] < r[:, None]))
+    rank = jnp.sum(ahead.astype(jnp.int32), axis=1)
     order = jnp.sum(jnp.where(rank[None, :] == r[:, None], r[None, :], 0), axis=1)
-    hot = prompt_group[:, None] == jnp.arange(GROUPS, dtype=jnp.int32)[None, :]
-    start = jnp.sum(jnp.where(hot, prompt_lens[None, :], 0), axis=1)
-    base = (start + tail_lens).astype(F32)
-    frequency = jnp.exp(jnp.arange(32, dtype=F32) * (-2.0 * math.log(150000.0) / 64))
-    angle = base[:, None] * jnp.tile(frequency, 4)[None, :]
-    cosb, sinb = jnp.cos(angle)[:, None, :], jnp.sin(angle)[:, None, :]
     freq = np.exp(np.arange(32) * (-2.0 * math.log(150000.0) / 64))
-    step_angle = (np.arange(16) % 4)[:, None] * np.tile(freq, 4)[None, :]
-    steps_cos = jnp.asarray(np.cos(step_angle), F32)
-    steps_sin = jnp.asarray(np.sin(step_angle), F32)
-    fresh = jnp.pad(fresh_key_value.reshape(12, 128), ((0, 4), (0, 0)))
-    own_ids = lax.dynamic_slice_in_dim(expert_ids, me * 3, 3, 0).reshape(12, 4)
-    own_ids = jnp.pad(own_ids, ((0, 4), (0, 0)), constant_values=-1)
-    routes = jnp.pad(route_weights.reshape(12, 4), ((0, 4), (0, 0)))
-    resid16 = jnp.pad(resid.reshape(12, D), ((0, 4), (0, 3072 - D)))
-    gain = jnp.pad(norm_gain, (0, 3072 - D)).reshape(1, 3072)
+    freq = np.tile(freq.astype(np.float32), 4)
+    step_angle = (np.arange(16) % 4)[:, None] * freq[None, :].astype(np.float64)
+    tables = np.zeros((40, 128), np.float32)
+    tables[0] = freq
+    tables[8:24] = np.cos(step_angle)
+    tables[24:40] = np.sin(step_angle)
+    fresh = fresh_key_value.transpose(0, 2, 1, 3).reshape(3, 4, 128)
+    ids = expert_ids.transpose(1, 2, 0)
+    gain = norm_gain.reshape(1, D)
     q = new_query.reshape(REQ, 4, 4, 128).transpose(0, 2, 1, 3).reshape(REQ, 16, 128)
     prompt = prompt_cache.transpose(0, 2, 1, 3).reshape(GROUPS, PBLOCK, 128)
     tail = decoded_tail_cache.transpose(0, 2, 1, 3).reshape(REQ, TBLOCK, 128)
@@ -536,17 +610,22 @@
     out = pl.pallas_call(
         layer_kernel,
         name="layer",
-        out_shape=jax.ShapeDtypeStruct((16, 3072), BF16),
-        in_specs=[smem] * 5 + [vmem] * 9 + [hbm] * 6,
+        out_shape=jax.ShapeDtypeStruct((3, 4, D), BF16),
+        in_specs=[smem] * 6 + [vmem] * 6 + [hbm] * 6,
         out_specs=vmem,
         scratch_shapes=[
             pltpu.VMEM((REQ, 16, 128), BF16),
             pltpu.VMEM((GROUPS, PBLOCK, 128), BF16),
             pltpu.VMEM((REQ, TBLOCK, 128), BF16),
             pltpu.VMEM((3072, 512), BF16),
-            pltpu.VMEM((2, FFL, D), BF16),
-            pltpu.VMEM((FFL, D), BF16),
-            pltpu.VMEM((FFL, CH), BF16),
+            pltpu.VMEM((2 * CH, D), BF16),
+            pltpu.VMEM((CH, D), BF16),
+            pltpu.VMEM((CH, CH), BF16),
+            pltpu.VMEM((REQ, 128), F32),
+            pltpu.VMEM((REQ, 128), F32),
+            pltpu.VMEM((16, 128), F32),
+            pltpu.VMEM((16, 128), F32),
+            pltpu.VMEM((16, 3072), F32),
             pltpu.VMEM((REQ, 32, 128), BF16),
             pltpu.VMEM((REQ, 16, 128), BF16),
             pltpu.VMEM((REQ, 16, 128), F32),
@@ -564,7 +643,7 @@
             pltpu.VMEM((N_SEQ, 16, 128), BF16),
             pltpu.VMEM((16, CH), BF16),
             pltpu.VMEM((N_HEAD, 16, CH), BF16),
-            pltpu.SemaphoreType.DMA((5,)),
+            pltpu.SemaphoreType.DMA((6,)),
             pltpu.SemaphoreType.DMA((GROUPS,)),
             seq_sem,
             seq_sem,
@@ -587,17 +666,15 @@
     )(
         order,
         rank,
+        prompt_group,
         tail_lens,
         prompt_lens,
         sinks,
-        cosb,
-        sinb,
-        steps_cos,
-        steps_sin,
+        jnp.asarray(tables),
         fresh,
-        own_ids,
-        routes,
-        resid16,
+        ids,
+        route_weights,
+        resid,
         gain,
         q,
         prompt,
@@ -606,7 +683,7 @@
         gu,
         dn,
     )
-    return out[:12, :D].reshape(3, 4, D)
+    return out
 
 
 def solution(mesh):

time: 100 us -> 90.3 us (0.903)
  local copies, waits for them, and re-layouts: 8.03 us -> 2.86 us
  other arithmetic: 4.99 us -> 1.55 us
  Pallas kernels: 86.7 us -> 85.7 us
    pad x5 -> x0, local copies, waits for them, and re-layouts: 3.75 us -> none  [the longest x1 1.31 us: on_device(): gain = jnp.pad(norm_gain, (0, 3072 - D)).reshape(1, 3072)]
    sin x1 -> x0, other arithmetic: 2.02 us -> none  [on_device(): cosb, sinb = (jnp.cos(angle)[:, None, :], jnp.sin(angle)[:, None, :])]
    reshape x6 -> x1, local copies, waits for them, and re-layouts: 3.14 us -> 1.31 us  [on_device(): gain = norm_gain.reshape(1, D)]
    unnamed x4 -> x3, local copies, waits for them, and re-layouts: 0.01 us -> 1.54 us
    pallas_call x1, Pallas kernels: 86.7 us -> 85.7 us  [on_device(): pl.pallas_call(layer_kernel, name='layer', out_shape=jax.ShapeDtypeStruct...]
where the time goes in v2:
time: 90.3 us; the launch traced here: 90.1 us
  Pallas kernels  85.7 us (95%)
  local copies, waits for them, and re-layouts  2.86 us (3%)
  other arithmetic  1.55 us (2%)
    pallas_call x1, Pallas kernels, on_device(): pl.pallas_call(layer_kernel, name='layer', out_shape=jax.ShapeDtypeStruct...  85.7 us

profile of v2, /device:TPU:1, one launch (start us, length us, event | category | flops | bytes accessed | tf_op | source)
XLA Modules:
  0.0 90.1 jit_solution(2956216657604728490)
XLA Ops:
  0.0 0.9 %convert_reduce_fusion.rank = s32[96]{0:T(128)S(1)} fusion(s32[96]{0:T(128)} %prompt_group.1), kind=kLoop, calls=%fused_computation.2 | loop fusion | flops 64416 | bytes 768 | tf_op jit(solution)/shard_map/reduce_sum | solution.py:586
  0.9 0.0 copy-start
  0.9 0.6 select_reduce_fusion.order
  1.6 1.3 %reshape.18.gain = f32[1,2880]{1,0:T(1,128)} reshape(f32[2880]{0:T(1024)} %param.26) | data formatting | bytes 23040 | tf_op jit(solution)/shard_map/reshape | solution.py:597
  2.9 0.0 copy-done
  2.9 85.7 %layer.1 = bf16[3,4,2880]{2,1,0:T(4,128)(2,1)} custom-call(s32[96]{0:T(128)} %select_reduce_fusion.order, s32[96]{0:T(128)} %copy-done, s32[96]{0:T(128)} %prompt_group.1, s32[96]{0:T(128)} %tail_lens.1, s32[8]{0:T(128)} %prompt_lens.1, f32[8]{0:T(128)} %sinks.1, f32[40,128]{1,0:T(8,128)} %constant.4.clone.tables, bf16[3,4,128]{2,1,0:T(4,128)(2,1)} %bitcast.21, ...), custom_call_target="tpu_custom_call" | custom-call | tf_op jit(solution)/shard_map/layer/pallas_call | solution.py:610
  88.6 1.5 %copy.20 = bf16[3,4,2880]{2,1,0:T(4,128)(2,1)} copy(bf16[3,4,2880]{2,1,0:T(4,128)(2,1)} %layer.1) | data formatting | bytes 138240
Async XLA Ops:
  0.9 2.0 %copy-start = (s32[96]{0:T(128)}, s32[96]{0:T(128)S(1)}, u32[]{:S(2)}) copy-start(s32[96]{0:T(128)S(1)} %convert_reduce_fusion.rank) | copy-start | bytes 1156

commit v3 on v2

--- a/solution.py
+++ b/solution.py
@@ -113,7 +113,13 @@
     small_s,
     route_s,
     resid_s,
+    both_s,
+    square_s,
     q_all,
+    even_s,
+    odd_s,
+    even_top,
+    odd_top,
     acc_s,
     stat_s,
     msg1,
@@ -205,8 +211,6 @@
 
     load_q.wait()
 
-    unit = jnp.where(lane == 64, 1.0, 0.0)
-
     def rotate_one(i, carry):
         r = order[i]
         x = q_v[r].astype(F32)
@@ -214,60 +218,89 @@
         s0 = sin_s[pl.ds(i, 1), :]
         y = turned(x, c0 * ct - s0 * st, s0 * ct + c0 * st, lane)
         y = y.astype(BF16).astype(F32) * 0.125
-        q_all[i, 0:16, :] = jnp.where(lane < 64, y, unit).astype(BF16)
+        q_all[i, 0:16, :] = jnp.where(lane < 64, y, 0.0).astype(BF16)
         q_all[i, 16:32, :] = jnp.where(
-            lane < 64, pltpu.roll(y, 64, 1), unit
+            lane < 64, pltpu.roll(y, 64, 1), 0.0
         ).astype(BF16)
         return carry
 
     lax.fori_loop(0, REQ, rotate_one, 0, unroll=4)
     load_tail.wait()
 
-    key_row = iota((PBLOCK, 128), 0) + me * PBLOCK
-    key_lane = iota((PBLOCK, 128), 1)
+    key_col = iota((1, PBLOCK), 1) + me * PBLOCK
     col128 = iota((1, 128), 1)
-    tail_lane = iota((128, 128), 1)
+    upper = (iota((1, 128), 1) >= 64).astype(F32).astype(BF16)
+    lower = (iota((1, 128), 1) < 64).astype(F32).astype(BF16)
     same_req = (iota((128, 128), 0) >> 5) == (iota((128, 128), 1) >> 5)
 
-    def one_group(g, carry):
-        load_prompt(g).wait()
-        first = g * MEMBERS
+    def tails(g):
+        members = [order[g * MEMBERS + i] for i in range(MEMBERS)]
+        return [
+            jnp.concatenate([tail_v[r] for r in members[4 * b : 4 * b + 4]], axis=0)
+            for b in range(3)
+        ], members
+
+    def scores(g, buf, tops):
         kv = prompt_v[g]
-        bias = jnp.where(key_row < prompt_lens[g], 0.0, LOW).astype(BF16)
-        kx = jnp.where(key_lane < 64, kv, bias)
-        vx = jnp.where(key_lane < 64, jnp.ones_like(kv), kv)
-        q = q_all[pl.ds(first, MEMBERS)].reshape(MEMBERS * 32, 128)
-        s = dot(q, kx, NT)
-        members = [order[first + i] for i in range(MEMBERS)]
-        s2 = []
-        vt = []
+        bias = jnp.where(key_col < prompt_lens[g], 0.0, LOW)
+        q = q_all[pl.ds(g * MEMBERS, MEMBERS)].reshape(MEMBERS * 32, 128)
+        high = None
+        for h in range(4):
+            cols = slice(256 * h, 256 * h + 256)
+            part = dot(q, kv[cols], NT) + bias[:, cols]
+            buf[:, cols] = part
+            part = jnp.maximum(part[:, :128], part[:, 128:])
+            high = part if high is None else jnp.maximum(high, part)
+        keys, members = tails(g)
         for b in range(3):
-            kt = jnp.concatenate([tail_v[r] for r in members[4 * b : 4 * b + 4]], axis=0)
+            rows = slice(128 * b, 128 * b + 128)
             limit = jnp.zeros((1, 128), jnp.int32)
             for i in range(4):
                 limit = jnp.where((col128 >> 5) == i, tail_lens[members[4 * b + i]], limit)
             seen = same_req & (((col128 & 31) + me * TBLOCK) < limit)
-            qt = jnp.where(tail_lane < 64, q[128 * b : 128 * b + 128], jnp.zeros_like(kt))
-            s2.append(jnp.where(seen, dot(qt, kt, NT), LOW))
-            vt.append(jnp.where(tail_lane < 64, jnp.ones_like(kt), kt))
-        s2 = jnp.concatenate(s2, axis=0)
-        peak = jnp.maximum(jnp.max(s, axis=1, keepdims=True), jnp.max(s2, axis=1, keepdims=True))
-        peak = jnp.maximum(peak, FLOOR).astype(BF16).astype(F32)
-        w = jnp.exp(s - peak).astype(BF16)
-        w2 = jnp.exp(s2 - peak).astype(BF16)
-        o = dot(w, vx, NN)
+            part = jnp.where(seen, dot(q[rows], keys[b], NT), LOW)
+            buf[rows, PBLOCK : PBLOCK + 128] = part
+            top = jnp.max(jnp.maximum(high[rows], part), axis=1, keepdims=True)
+            top = jnp.maximum(top, FLOOR).astype(BF16).astype(F32)
+            tops[rows, :] = jnp.broadcast_to(top, (128, 128))
+
+    def weigh(g, buf, tops):
+        first = g * MEMBERS
+        kv = prompt_v[g]
+        vx = kv * upper + lower
+        keys, members = tails(g)
+        peaks = tops[...]
+        w = jnp.concatenate(
+            [
+                jnp.exp(buf[:, 128 * h : 128 * h + 128] - peaks).astype(BF16)
+                for h in range(PBLOCK // 128)
+            ],
+            axis=1,
+        )
+        w2 = jnp.exp(buf[:, PBLOCK : PBLOCK + 128] - peaks).astype(BF16)
+        whole = dot(w, vx, NN)
         for b in range(3):
-            ob = o[128 * b : 128 * b + 128] + dot(w2[128 * b : 128 * b + 128], vt[b], NN)
-            pb = peak[128 * b : 128 * b + 128]
+            rows = slice(128 * b, 128 * b + 128)
+            peak = peaks[rows]
+            o = whole[rows] + dot(w2[rows], keys[b] * upper + lower, NN)
             for i in range(4):
-                values, stats = tiles_of(
-                    ob[32 * i : 32 * i + 32], pb[32 * i : 32 * i + 32], lane
-                )
+                values, stats = tiles_of(o[32 * i : 32 * i + 32], peak[32 * i : 32 * i + 32], lane)
                 acc_s[first + 4 * b + i] = values
                 stat_s[first + 4 * b + i] = stats
+
+    for g in range(GROUPS):
+        load_prompt(g).wait()
+    scores(0, even_s, even_top)
+
+    def two_groups(k, carry):
+        g = 2 * k
+        scores(g + 1, odd_s, odd_top)
+        weigh(g, even_s, even_top)
+        scores(jnp.minimum(g + 2, GROUPS - 1), even_s, even_top)
+        weigh(g + 1, odd_s, odd_top)
         return carry
 
-    lax.fori_loop(0, GROUPS, one_group, 0)
+    lax.fori_loop(0, GROUPS // 2, two_groups, 0)
 
     pl.semaphore_wait(barrier, N_SEQ - 1 + N_HEAD - 1)
 
@@ -326,6 +359,13 @@
             return carry
 
         lax.fori_loop(1, count, step, 0)
+
+    core = lax.rem(head, 2)
+    chip = head // 2
+    near = chip + 1 - 2 * lax.rem(chip, 2)
+    peers = [2 * chip + 1 - core]
+    for far in (near, 3 - chip, lax.rem(chip + 2, 4)):
+        peers += [2 * far + core, 2 * far + 1 - core]
 
     def send_partials(o):
         pack(msg1, o, o)
@@ -351,7 +391,6 @@
         k = rank[3 * me + i]
         q = q_all[k]
         seen = ((scol >> 2) == i) & ((scol & 3) <= (srow & 3))
-        q = jnp.where(iota((32, 128), 1) < 64, q, jnp.zeros_like(q))
         s = jnp.where(seen, dot(q, kn, NT), LOW)
         peak = jnp.max(s, axis=1, keepdims=True).astype(BF16).astype(F32)
         w = jnp.exp(s - peak).astype(BF16)
@@ -483,22 +522,31 @@
     others(N_HEAD, head, lambda o: head_copy(msg4, None, rcv4, send4, recv4, o).start())
     rcv4[head] = mine
 
-    both = jnp.zeros((ROWS, 2 * CH), F32)
-    square = jnp.zeros((ROWS, 1), F32)
-    for half in range(2):
-        parts = []
-        for j in range(4 * half, 4 * half + 4):
-
-            @pl.when(head != j)
-            def _():
-                head_arrival(msg4, None, rcv4, send4, recv4, j).wait_recv()
-
-            width = CH if j < N_HEAD - 1 else LASTC
-            x = rcv4[j, :, 0:width].astype(F32)
-            square = square + jnp.sum(x * x, axis=1, keepdims=True)
-            parts.append((x * gain[:, j * CH : j * CH + width]).astype(BF16))
-        stop = min(D, 4 * (half + 1) * CH)
-        both = both + dot(jnp.concatenate(parts, axis=1), gu_v[:, 4 * half * CH : stop], NT)
+    both_s[...] = jnp.zeros((ROWS, 2 * CH), F32)
+    square_s[...] = jnp.zeros((ROWS, 128), F32)
+
+    def take_chunk(j, weights, width, gains):
+        x = rcv4[j, :, 0:width].astype(F32)
+        square_s[...] += jnp.broadcast_to(jnp.sum(x * x, axis=1, keepdims=True), (ROWS, 128))
+        both_s[...] += dot((x * gains).astype(BF16), weights, NT)
+
+    def use_chunk(j):
+        @pl.when(j < N_HEAD - 1)
+        def _():
+            cols = pl.ds(pl.multiple_of(jnp.minimum(j, N_HEAD - 2) * CH, CH), CH)
+            take_chunk(j, gu_v[:, cols], CH, gain[:, cols])
+
+        @pl.when(j == N_HEAD - 1)
+        def _():
+            cols = slice((N_HEAD - 1) * CH, D)
+            take_chunk(N_HEAD - 1, gu_v[:, cols], LASTC, gain[:, cols])
+
+    use_chunk(head)
+    for j in peers:
+        head_arrival(msg4, None, rcv4, send4, recv4, j).wait_recv()
+        use_chunk(j)
+    both = both_s[...]
+    square = square_s[:, 0:1]
     scale = lax.rsqrt(square * (1.0 / D) + 1e-05)
     g = jnp.minimum(both[:, 0:CH] * scale, 7.0)
     u = jnp.clip(both[:, CH : 2 * CH] * scale, -7.0, 7.0)
@@ -626,7 +674,13 @@
             pltpu.VMEM((16, 128), F32),
             pltpu.VMEM((16, 128), F32),
             pltpu.VMEM((16, 3072), F32),
+            pltpu.VMEM((ROWS, 2 * CH), F32),
+            pltpu.VMEM((ROWS, 128), F32),
             pltpu.VMEM((REQ, 32, 128), BF16),
+            pltpu.VMEM((MEMBERS * 32, PBLOCK + 128), F32),
+            pltpu.VMEM((MEMBERS * 32, PBLOCK + 128), F32),
+            pltpu.VMEM((MEMBERS * 32, 128), F32),
+            pltpu.VMEM((MEMBERS * 32, 128), F32),
             pltpu.VMEM((REQ, 16, 128), BF16),
             pltpu.VMEM((REQ, 16, 128), F32),
             pltpu.VMEM((N_SEQ, 64, 128), BF16),

time: 90.3 us -> 85.7 us (0.949)
  Pallas kernels: 85.7 us -> 81 us
    pallas_call x1, Pallas kernels: 85.7 us -> 81 us  [on_device(): pl.pallas_call(layer_kernel, name='layer', out_shape=jax.ShapeDtypeStruct...]
where the time goes in v3:
time: 85.7 us; the launch traced here: 85.5 us
  Pallas kernels  81 us (95%)
  local copies, waits for them, and re-layouts  2.86 us (3%)
  other arithmetic  1.55 us (2%)
    pallas_call x1, Pallas kernels, on_device(): pl.pallas_call(layer_kernel, name='layer', out_shape=jax.ShapeDtypeStruct...  81 us

profile of v3, /device:TPU:1, one launch (start us, length us, event | category | flops | bytes accessed | tf_op | source)
XLA Modules:
  0.0 85.5 jit_solution(10020598438656946672)
XLA Ops:
  0.0 0.9 %convert_reduce_fusion.rank = s32[96]{0:T(128)S(1)} fusion(s32[96]{0:T(128)} %prompt_group.1), kind=kLoop, calls=%fused_computation.2 | loop fusion | flops 64416 | bytes 768 | tf_op jit(solution)/shard_map/reduce_sum | solution.py:634
  0.9 0.0 copy-start
  0.9 0.6 select_reduce_fusion.order
  1.6 1.3 %reshape.18.gain = f32[1,2880]{1,0:T(1,128)} reshape(f32[2880]{0:T(1024)} %param.26) | data formatting | bytes 23040 | tf_op jit(solution)/shard_map/reshape | solution.py:645
  2.9 0.0 copy-done
  2.9 81.0 %layer.1 = bf16[3,4,2880]{2,1,0:T(4,128)(2,1)} custom-call(s32[96]{0:T(128)} %select_reduce_fusion.order, s32[96]{0:T(128)} %copy-done, s32[96]{0:T(128)} %prompt_group.1, s32[96]{0:T(128)} %tail_lens.1, s32[8]{0:T(128)} %prompt_lens.1, f32[8]{0:T(128)} %sinks.1, f32[40,128]{1,0:T(8,128)} %constant.4.clone.tables, bf16[3,4,128]{2,1,0:T(4,128)(2,1)} %bitcast.21, ...), custom_call_target="tpu_custom_call" | custom-call | tf_op jit(solution)/shard_map/layer/pallas_call | solution.py:658
  83.9 1.5 %copy.20 = bf16[3,4,2880]{2,1,0:T(4,128)(2,1)} copy(bf16[3,4,2880]{2,1,0:T(4,128)(2,1)} %layer.1) | data formatting | bytes 138240
Async XLA Ops:
  0.9 2.0 %copy-start = (s32[96]{0:T(128)}, s32[96]{0:T(128)S(1)}, u32[]{:S(2)}) copy-start(s32[96]{0:T(128)S(1)} %convert_reduce_fusion.rank) | copy-start | bytes 1156

commit v4 on v3

--- a/solution.py
+++ b/solution.py
@@ -107,7 +107,9 @@
     ow_v,
     gu_v,
     dn_v,
-    dn_last,
+    dn_w,
+    gu_w,
+    gain_s,
     cos_s,
     sin_s,
     small_s,
@@ -130,6 +132,8 @@
     rcv3,
     msg4,
     rcv4,
+    msg_p,
+    rcv_p,
     msg5,
     rcv5,
     msg6,
@@ -146,6 +150,9 @@
     recv3,
     send4,
     recv4,
+    send_f,
+    send_p,
+    recv_p,
     send5,
     recv5,
     send6,
@@ -311,7 +318,7 @@
             dst[slot, 16 * i : 16 * i + 16, :] = acc_s[k]
             piece = stat_s[k]
             total = total + (piece if i == 0 else pltpu.roll(piece, 8 * i, 1))
-        dst[slot, 48:64, :] = total.astype(BF16)
+        dst[slot, 48:56, :] = (total[:8] + pltpu.roll(total[8:], 64, 1)).astype(BF16)
 
     def seq_copy(msg, rcv, send, recv, to):
         return pltpu.make_async_remote_copy(
@@ -363,9 +370,8 @@
     core = lax.rem(head, 2)
     chip = head // 2
     near = chip + 1 - 2 * lax.rem(chip, 2)
-    peers = [2 * chip + 1 - core]
-    for far in (near, 3 - chip, lax.rem(chip + 2, 4)):
-        peers += [2 * far + core, 2 * far + 1 - core]
+    sibling = 2 * chip + 1 - core
+    far = [near, 3 - chip, lax.rem(chip + 2, 4)]
 
     def send_partials(o):
         pack(msg1, o, o)
@@ -397,7 +403,8 @@
         values, stats = tiles_of(dot(w, vn, NN), peak, lane)
         rcv1[N_SEQ, 16 * i : 16 * i + 16, :] = values
         fresh_stats = fresh_stats + (stats if i == 0 else pltpu.roll(stats, 8 * i, 1))
-    rcv1[N_SEQ, 48:64, :] = fresh_stats.astype(BF16)
+    folded = fresh_stats[:8] + pltpu.roll(fresh_stats[8:], 64, 1)
+    rcv1[N_SEQ, 48:56, :] = folded.astype(BF16)
 
     sink = jnp.zeros((16, 128), F32)
     for j in range(8):
@@ -467,28 +474,35 @@
     gu_v[FFL:CH, :] = jnp.zeros((CH - FFL, D), BF16)
     gu_v[CH + FFL : 2 * CH, :] = jnp.zeros((CH - FFL, D), BF16)
     dn_v[FFL:CH, :] = jnp.zeros((CH - FFL, D), BF16)
-    dn_last[:, 0:LASTC] = dn_v[:, 7 * CH : 7 * CH + LASTC]
-    dn_last[:, LASTC:CH] = jnp.zeros((CH, CH - LASTC), BF16)
+    dn_w[:, 2816:3072] = jnp.zeros((CH, 256), BF16)
+    dn_w[:, 0:D] = dn_v[...]
+    gu_w[:, 2816:3072] = jnp.zeros((2 * CH, 256), BF16)
+    gu_w[:, 0:D] = gu_v[...]
+    gain_s[:, 2816:3072] = jnp.zeros((1, 256), F32)
+    gain_s[:, 0:D] = gain[...]
 
     others(N_SEQ, me, lambda s: seq_arrival(msg1, rcv1, send1, recv1, s).wait_recv())
 
-    stat_rows = rcv1[:, 48:64, :].reshape((N_SEQ + 1) * 16, 128)
+    stat_rows = rcv1[:, 48:56, :].reshape((N_SEQ + 1) * 8, 128)
     er = iota((128, 384), 0)
     ec = iota((128, 384), 1)
     attended = []
     for i in range(3):
-        spot = 8 * i + 4 * ((ec & 127) >> 6) + (ec >> 7)
-        expand = (er == spot).astype(F32).astype(BF16)
-        wide = dot(stat_rows, expand, NN)
-        peaks = wide[:, 0:128].reshape(N_SEQ + 1, 16, 128)
-        totals = (wide[:, 128:256] + wide[:, 256:384]).reshape(N_SEQ + 1, 16, 128)
-        top = jnp.maximum(jnp.max(peaks, axis=0), sink)
-        factor = jnp.exp(peaks - top[None])
-        values = rcv1[:, 16 * i : 16 * i + 16, :].astype(F32)
-        num = jnp.sum(values * factor, axis=0)
-        den = jnp.sum(totals * factor, axis=0) + jnp.exp(sink - top)
-        attended.append((num / den).astype(BF16))
-    att = jnp.concatenate(attended, axis=0)
+        for half in range(2):
+            spot = 64 * half + 8 * i + 4 * ((ec & 127) >> 6) + (ec >> 7)
+            expand = (er == spot).astype(F32).astype(BF16)
+            wide = dot(stat_rows, expand, NN)
+            peaks = wide[:, 0:128].reshape(N_SEQ + 1, 8, 128)
+            totals = (wide[:, 128:256] + wide[:, 256:384]).reshape(N_SEQ + 1, 8, 128)
+            sunk = sink[8 * half : 8 * half + 8]
+            top = jnp.maximum(jnp.max(peaks, axis=0), sunk)
+            factor = jnp.exp(peaks - top[None])
+            start = 16 * i + 8 * half
+            values = rcv1[:, start : start + 8, :].astype(F32)
+            num = jnp.sum(values * factor, axis=0)
+            den = jnp.sum(totals * factor, axis=0) + jnp.exp(sunk - top)
+            attended.append(num / den)
+    att = jnp.concatenate(attended, axis=0).astype(BF16)
     rr = iota((64, 48), 0)
     rc = iota((64, 48), 1)
     want = ((rr & 15) >> 2) * 16 + (rr >> 4) * 4 + (rr & 3)
@@ -519,31 +533,41 @@
     got = dot(spread, rcv3[...].reshape(512, 128), NN).astype(BF16)
     mine = jnp.concatenate([got[96 * c : 96 * c + 96] for c in range(3)], axis=1)
     msg4[...] = mine
-    others(N_HEAD, head, lambda o: head_copy(msg4, None, rcv4, send4, recv4, o).start())
+    gather_to = [2 * far[2] + core, 2 * far[0] + core, 2 * far[1] + core, sibling]
+    for j in gather_to:
+        head_copy(msg4, None, rcv4, send4, recv4, j).start()
     rcv4[head] = mine
 
     both_s[...] = jnp.zeros((ROWS, 2 * CH), F32)
     square_s[...] = jnp.zeros((ROWS, 128), F32)
 
-    def take_chunk(j, weights, width, gains):
-        x = rcv4[j, :, 0:width].astype(F32)
+    def use_chunk(j):
+        cols = pl.ds(pl.multiple_of(j * CH, CH), CH)
+        x = rcv4[j].astype(F32)
         square_s[...] += jnp.broadcast_to(jnp.sum(x * x, axis=1, keepdims=True), (ROWS, 128))
-        both_s[...] += dot((x * gains).astype(BF16), weights, NT)
-
-    def use_chunk(j):
-        @pl.when(j < N_HEAD - 1)
-        def _():
-            cols = pl.ds(pl.multiple_of(jnp.minimum(j, N_HEAD - 2) * CH, CH), CH)
-            take_chunk(j, gu_v[:, cols], CH, gain[:, cols])
-
-        @pl.when(j == N_HEAD - 1)
-        def _():
-            cols = slice((N_HEAD - 1) * CH, D)
-            take_chunk(N_HEAD - 1, gu_v[:, cols], LASTC, gain[:, cols])
+        both_s[...] += dot((x * gain_s[:, cols]).astype(BF16), gu_w[:, cols], NT)
+
+    def forward(k, j):
+        return pltpu.make_async_remote_copy(
+            src_ref=rcv4.at[j],
+            dst_ref=rcv4.at[j],
+            send_sem=send_f.at[k],
+            recv_sem=recv4.at[j],
+            device_id=(me, sibling),
+            device_id_type=MESH,
+        )
 
     use_chunk(head)
-    for j in peers:
+    head_arrival(msg4, None, rcv4, send4, recv4, sibling).wait_recv()
+    use_chunk(sibling)
+    for k in range(3):
+        j = 2 * far[k] + core
         head_arrival(msg4, None, rcv4, send4, recv4, j).wait_recv()
+        forward(k, j).start()
+        use_chunk(j)
+    for k in range(3):
+        j = 2 * far[k] + 1 - core
+        forward(k, j).wait_recv()
         use_chunk(j)
     both = both_s[...]
     square = square_s[:, 0:1]
@@ -552,27 +576,44 @@
     u = jnp.clip(both[:, CH : 2 * CH] * scale, -7.0, 7.0)
     active = ((u + 1.0) * g * jax.nn.sigmoid(1.702 * g)).astype(BF16)
 
-    def send_expert(d, carry):
-        j = lax.rem(head + d, N_HEAD)
-        col = pl.multiple_of(jnp.minimum(j, N_HEAD - 2) * CH, CH)
-
-        @pl.when(j < N_HEAD - 1)
-        def _():
-            msg5[j] = dot(active, dn_v[:, pl.ds(col, CH)], NN).astype(BF16)
-
-        @pl.when(j == N_HEAD - 1)
-        def _():
-            msg5[j] = dot(active, dn_last[...], NN).astype(BF16)
-
-        @pl.when(d < N_HEAD)
-        def _():
-            head_copy(msg5, j, rcv5, send5, recv5, j).start()
-
-        return carry
-
-    lax.fori_loop(1, N_HEAD + 1, send_expert, 0)
-    rcv5[head] = msg5[head]
-    others(N_HEAD, head, lambda s: head_arrival(msg5, s, rcv5, send5, recv5, s).wait_recv())
+    def product(j):
+        return dot(active, dn_w[:, pl.ds(pl.multiple_of(j * CH, CH), CH)], NN)
+
+    def pair_copy(c):
+        return pltpu.make_async_remote_copy(
+            src_ref=msg_p.at[c],
+            dst_ref=rcv_p.at[c],
+            send_sem=send_p.at[c],
+            recv_sem=recv_p.at[c],
+            device_id=(me, sibling),
+            device_id_type=MESH,
+        )
+
+    def chip_copy(c, slot):
+        return pltpu.make_async_remote_copy(
+            src_ref=msg5.at[c],
+            dst_ref=rcv5.at[slot],
+            send_sem=send5.at[c],
+            recv_sem=recv5.at[slot],
+            device_id=(me, 2 * c + core),
+            device_id_type=MESH,
+        )
+
+    turns = [far[2], far[0], far[1], chip]
+    for c in turns:
+        msg_p[c] = product(2 * c + 1 - core).astype(BF16)
+        pair_copy(c).start()
+    for k, c in enumerate(turns):
+        own = product(2 * c + core)
+        pair_copy(c).wait_recv()
+        both_cores = (own + rcv_p[c].astype(F32)).astype(BF16)
+        if k < 3:
+            msg5[c] = both_cores
+            chip_copy(c, chip).start()
+        else:
+            rcv5[chip] = both_cores
+    for c in far:
+        chip_copy(c, c).wait_recv()
     summed = jnp.sum(rcv5[...].astype(F32), axis=0).astype(BF16)
     summed_rows = jnp.concatenate([summed[:, 128 * c : 128 * c + 128] for c in range(3)], axis=0)
     msg6[...] = dot(gather, summed_rows, NN).astype(BF16).reshape(N_SEQ, 16, 128)
@@ -598,17 +639,16 @@
         (msg6, rcv6, send6, recv6),
     ):
         others(N_SEQ, me, lambda o: seq_copy(msg, rcv, send, recv, o).wait_send())
-    for msg, whole, rcv, send, recv in (
-        (msg2, False, rcv2, send2, recv2),
-        (msg4, True, rcv4, send4, recv4),
-        (msg5, False, rcv5, send5, recv5),
-        (msg7, True, rcv7, send7, recv7),
-    ):
-        others(
-            N_HEAD,
-            head,
-            lambda o: head_copy(msg, None if whole else o, rcv, send, recv, o).wait_send(),
-        )
+    for j in gather_to:
+        head_copy(msg4, None, rcv4, send4, recv4, j).wait_send()
+    for k in range(3):
+        forward(k, 2 * far[k] + core).wait_send()
+    for k, c in enumerate(turns):
+        pair_copy(c).wait_send()
+        if k < 3:
+            chip_copy(c, chip).wait_send()
+    others(N_HEAD, head, lambda o: head_copy(msg2, o, rcv2, send2, recv2, o).wait_send())
+    others(N_HEAD, head, lambda o: head_copy(msg7, None, rcv7, send7, recv7, o).wait_send())
 
 
 def on_device(
@@ -655,6 +695,7 @@
     hbm = pl.BlockSpec(memory_space=pl.ANY)
     seq_sem = pltpu.SemaphoreType.DMA((N_SEQ,))
     head_sem = pltpu.SemaphoreType.DMA((N_HEAD,))
+    chip_sem = pltpu.SemaphoreType.DMA((4,))
     out = pl.pallas_call(
         layer_kernel,
         name="layer",
@@ -668,7 +709,9 @@
             pltpu.VMEM((3072, 512), BF16),
             pltpu.VMEM((2 * CH, D), BF16),
             pltpu.VMEM((CH, D), BF16),
-            pltpu.VMEM((CH, CH), BF16),
+            pltpu.VMEM((CH, 3072), BF16),
+            pltpu.VMEM((2 * CH, 3072), BF16),
+            pltpu.VMEM((1, 3072), F32),
             pltpu.VMEM((REQ, 128), F32),
             pltpu.VMEM((REQ, 128), F32),
             pltpu.VMEM((16, 128), F32),
@@ -683,16 +726,18 @@
             pltpu.VMEM((MEMBERS * 32, 128), F32),
             pltpu.VMEM((REQ, 16, 128), BF16),
             pltpu.VMEM((REQ, 16, 128), F32),
-            pltpu.VMEM((N_SEQ, 64, 128), BF16),
-            pltpu.VMEM((N_SEQ + 1, 64, 128), BF16),
+            pltpu.VMEM((N_SEQ, 56, 128), BF16),
+            pltpu.VMEM((N_SEQ + 1, 56, 128), BF16),
             pltpu.VMEM((N_HEAD, 16, CH), BF16),
             pltpu.VMEM((N_HEAD, 16, CH), BF16),
             pltpu.VMEM((N_SEQ, 16, 128), BF16),
             pltpu.VMEM((N_SEQ, 16, 128), BF16),
             pltpu.VMEM((ROWS, CH), BF16),
             pltpu.VMEM((N_HEAD, ROWS, CH), BF16),
-            pltpu.VMEM((N_HEAD, ROWS, CH), BF16),
-            pltpu.VMEM((N_HEAD, ROWS, CH), BF16),
+            pltpu.VMEM((4, ROWS, CH), BF16),
+            pltpu.VMEM((4, ROWS, CH), BF16),
+            pltpu.VMEM((4, ROWS, CH), BF16),
+            pltpu.VMEM((4, ROWS, CH), BF16),
             pltpu.VMEM((N_SEQ, 16, 128), BF16),
             pltpu.VMEM((N_SEQ, 16, 128), BF16),
             pltpu.VMEM((16, CH), BF16),
@@ -707,8 +752,11 @@
             seq_sem,
             head_sem,
             head_sem,
-            head_sem,
-            head_sem,
+            chip_sem,
+            chip_sem,
+            chip_sem,
+            chip_sem,
+            chip_sem,
             seq_sem,
             seq_sem,
             head_sem,

time: 85.7 us -> 81 us (0.945)
  Pallas kernels: 81 us -> 76.4 us
    pallas_call x1, Pallas kernels: 81 us -> 76.4 us  [on_device(): pl.pallas_call(layer_kernel, name='layer', out_shape=jax.ShapeDtypeStruct...]
where the time goes in v4:
time: 81 us; the launch traced here: 80.8 us
  Pallas kernels  76.4 us (94%)
  local copies, waits for them, and re-layouts  2.86 us (4%)
  other arithmetic  1.55 us (2%)
    pallas_call x1, Pallas kernels, on_device(): pl.pallas_call(layer_kernel, name='layer', out_shape=jax.ShapeDtypeStruct...  76.4 us

profile of v4, /device:TPU:1, one launch (start us, length us, event | category | flops | bytes accessed | tf_op | source)
XLA Modules:
  0.0 80.8 jit_solution(4169446449641274713)
XLA Ops:
  0.0 0.9 %convert_reduce_fusion.rank = s32[96]{0:T(128)S(1)} fusion(s32[96]{0:T(128)} %prompt_group.1), kind=kLoop, calls=%fused_computation.2 | loop fusion | flops 64416 | bytes 768 | tf_op jit(solution)/shard_map/reduce_sum | solution.py:674
  0.9 0.0 copy-start
  0.9 0.6 select_reduce_fusion.order
  1.6 1.3 %reshape.18.gain = f32[1,2880]{1,0:T(1,128)} reshape(f32[2880]{0:T(1024)} %param.26) | data formatting | bytes 23040 | tf_op jit(solution)/shard_map/reshape | solution.py:685
  2.9 0.0 copy-done
  2.9 76.4 %layer.1 = bf16[3,4,2880]{2,1,0:T(4,128)(2,1)} custom-call(s32[96]{0:T(128)} %select_reduce_fusion.order, s32[96]{0:T(128)} %copy-done, s32[96]{0:T(128)} %prompt_group.1, s32[96]{0:T(128)} %tail_lens.1, s32[8]{0:T(128)} %prompt_lens.1, f32[8]{0:T(128)} %sinks.1, f32[40,128]{1,0:T(8,128)} %constant.4.clone.tables, bf16[3,4,128]{2,1,0:T(4,128)(2,1)} %bitcast.21, ...), custom_call_target="tpu_custom_call" | custom-call | tf_op jit(solution)/shard_map/layer/pallas_call | solution.py:699
  79.3 1.5 %copy.20 = bf16[3,4,2880]{2,1,0:T(4,128)(2,1)} copy(bf16[3,4,2880]{2,1,0:T(4,128)(2,1)} %layer.1) | data formatting | bytes 138240
Async XLA Ops:
  0.9 2.0 %copy-start = (s32[96]{0:T(128)}, s32[96]{0:T(128)S(1)}, u32[]{:S(2)}) copy-start(s32[96]{0:T(128)S(1)} %convert_reduce_fusion.rank) | copy-start | bytes 1156

commit v5 on v4

--- a/solution.py
+++ b/solution.py
@@ -65,20 +65,16 @@
 
 
 def tiles_of(out, peak, lane):
-    first, second = out[:16], out[16:]
+    first, second = out[:8], out[8:]
     values = jnp.where(lane < 64, pltpu.roll(first, 64, 1), second).astype(BF16)
     hi0 = first.astype(BF16).astype(F32)
     hi1 = second.astype(BF16).astype(F32)
     lo0 = first - hi0
     lo1 = second - hi1
-    stats = jnp.where(
-        lane < 4,
-        jnp.where(lane == 0, peak[:16], jnp.where(lane == 1, hi0, jnp.where(lane == 2, lo0, 0.0))),
-        jnp.where(
-            lane == 4, peak[16:], jnp.where(lane == 5, hi1, jnp.where(lane == 6, lo1, 0.0))
-        ),
-    )
-    return values, jnp.where(lane < 8, stats, 0.0)
+    left = jnp.where(lane == 0, peak[:8], jnp.where(lane == 1, hi0, lo0))
+    right = jnp.where(lane == 4, peak[8:], jnp.where(lane == 5, hi1, lo1))
+    stats = jnp.where(lane < 3, left, jnp.where((lane >= 4) & (lane < 7), right, 0.0))
+    return values, stats
 
 
 def layer_kernel(
@@ -113,6 +109,7 @@
     cos_s,
     sin_s,
     small_s,
+    att_s,
     route_s,
     resid_s,
     both_s,
@@ -142,6 +139,8 @@
     rcv7,
     load_sem,
     prompt_sem,
+    send0,
+    recv0,
     send1,
     recv1,
     send2,
@@ -225,10 +224,11 @@
         s0 = sin_s[pl.ds(i, 1), :]
         y = turned(x, c0 * ct - s0 * st, s0 * ct + c0 * st, lane)
         y = y.astype(BF16).astype(F32) * 0.125
-        q_all[i, 0:16, :] = jnp.where(lane < 64, y, 0.0).astype(BF16)
-        q_all[i, 16:32, :] = jnp.where(
-            lane < 64, pltpu.roll(y, 64, 1), 0.0
-        ).astype(BF16)
+        even = jnp.where(lane < 64, y, 0.0)
+        odd = jnp.where(lane < 64, pltpu.roll(y, 64, 1), 0.0)
+        for h in range(2):
+            part = slice(8 * h, 8 * h + 8)
+            q_all[h * REQ + i] = jnp.concatenate([even[part], odd[part]], axis=0).astype(BF16)
         return carry
 
     lax.fori_loop(0, REQ, rotate_one, 0, unroll=4)
@@ -238,7 +238,8 @@
     col128 = iota((1, 128), 1)
     upper = (iota((1, 128), 1) >= 64).astype(F32).astype(BF16)
     lower = (iota((1, 128), 1) < 64).astype(F32).astype(BF16)
-    same_req = (iota((128, 128), 0) >> 5) == (iota((128, 128), 1) >> 5)
+    same_req = (iota((64, 128), 0) >> 4) == (iota((64, 128), 1) >> 5)
+    lane8 = lane[:8]
 
     def tails(g):
         members = [order[g * MEMBERS + i] for i in range(MEMBERS)]
@@ -247,10 +248,11 @@
             for b in range(3)
         ], members
 
-    def scores(g, buf, tops):
+    def scores(n, buf, tops):
+        g = lax.rem(n, GROUPS)
         kv = prompt_v[g]
         bias = jnp.where(key_col < prompt_lens[g], 0.0, LOW)
-        q = q_all[pl.ds(g * MEMBERS, MEMBERS)].reshape(MEMBERS * 32, 128)
+        q = q_all[pl.ds(n * MEMBERS, MEMBERS)].reshape(MEMBERS * 16, 128)
         high = None
         for h in range(4):
             cols = slice(256 * h, 256 * h + 256)
@@ -260,7 +262,7 @@
             high = part if high is None else jnp.maximum(high, part)
         keys, members = tails(g)
         for b in range(3):
-            rows = slice(128 * b, 128 * b + 128)
+            rows = slice(64 * b, 64 * b + 64)
             limit = jnp.zeros((1, 128), jnp.int32)
             for i in range(4):
                 limit = jnp.where((col128 >> 5) == i, tail_lens[members[4 * b + i]], limit)
@@ -269,10 +271,11 @@
             buf[rows, PBLOCK : PBLOCK + 128] = part
             top = jnp.max(jnp.maximum(high[rows], part), axis=1, keepdims=True)
             top = jnp.maximum(top, FLOOR).astype(BF16).astype(F32)
-            tops[rows, :] = jnp.broadcast_to(top, (128, 128))
-
-    def weigh(g, buf, tops):
-        first = g * MEMBERS
+            tops[rows, :] = jnp.broadcast_to(top, (64, 128))
+
+    def weigh(n, buf, tops):
+        g = lax.rem(n, GROUPS)
+        first = n * MEMBERS
         kv = prompt_v[g]
         vx = kv * upper + lower
         keys, members = tails(g)
@@ -287,11 +290,13 @@
         w2 = jnp.exp(buf[:, PBLOCK : PBLOCK + 128] - peaks).astype(BF16)
         whole = dot(w, vx, NN)
         for b in range(3):
-            rows = slice(128 * b, 128 * b + 128)
+            rows = slice(64 * b, 64 * b + 64)
             peak = peaks[rows]
             o = whole[rows] + dot(w2[rows], keys[b] * upper + lower, NN)
             for i in range(4):
-                values, stats = tiles_of(o[32 * i : 32 * i + 32], peak[32 * i : 32 * i + 32], lane)
+                values, stats = tiles_of(
+                    o[16 * i : 16 * i + 16], peak[16 * i : 16 * i + 16], lane8
+                )
                 acc_s[first + 4 * b + i] = values
                 stat_s[first + 4 * b + i] = stats
 
@@ -299,26 +304,26 @@
         load_prompt(g).wait()
     scores(0, even_s, even_top)
 
-    def two_groups(k, carry):
-        g = 2 * k
-        scores(g + 1, odd_s, odd_top)
-        weigh(g, even_s, even_top)
-        scores(jnp.minimum(g + 2, GROUPS - 1), even_s, even_top)
-        weigh(g + 1, odd_s, odd_top)
+    def two_steps(k, carry):
+        n = 2 * k
+        scores(n + 1, odd_s, odd_top)
+        weigh(n, even_s, even_top)
+        scores(jnp.minimum(n + 2, 2 * GROUPS - 1), even_s, even_top)
+        weigh(n + 1, odd_s, odd_top)
         return carry
 
-    lax.fori_loop(0, GROUPS // 2, two_groups, 0)
+    lax.fori_loop(0, GROUPS // 2, two_steps, 0)
 
     pl.semaphore_wait(barrier, N_SEQ - 1 + N_HEAD - 1)
 
-    def pack(dst, slot, o):
-        total = jnp.zeros((16, 128), F32)
+    def pack(dst, half, slot, o):
+        total = jnp.zeros((8, 128), F32)
         for i in range(3):
-            k = rank[3 * o + i]
-            dst[slot, 16 * i : 16 * i + 16, :] = acc_s[k]
+            k = half * REQ + rank[3 * o + i]
+            dst[half, slot, 8 * i : 8 * i + 8, :] = acc_s[k]
             piece = stat_s[k]
             total = total + (piece if i == 0 else pltpu.roll(piece, 8 * i, 1))
-        dst[slot, 48:56, :] = (total[:8] + pltpu.roll(total[8:], 64, 1)).astype(BF16)
+        dst[half, slot, 24:32, :] = total.astype(BF16)
 
     def seq_copy(msg, rcv, send, recv, to):
         return pltpu.make_async_remote_copy(
@@ -373,12 +378,21 @@
     sibling = 2 * chip + 1 - core
     far = [near, 3 - chip, lax.rem(chip + 2, 4)]
 
-    def send_partials(o):
-        pack(msg1, o, o)
-        seq_copy(msg1, rcv1, send1, recv1, o).start()
-
-    others(N_SEQ, me, send_partials)
-    pack(rcv1, me, me)
+    def exchange(half):
+        sends, recvs = (send1, recv1) if half == 0 else (send0, recv0)
+        return msg1.at[half], rcv1.at[half], sends, recvs
+
+    def send_partials(half):
+        def one(o):
+            pack(msg1, half, o, o)
+            seq_copy(*exchange(half), o).start()
+
+        others(N_SEQ, me, one)
+        pack(rcv1, half, me, me)
+
+    send_partials(0)
+    lax.fori_loop(GROUPS // 2, GROUPS, two_steps, 0)
+    send_partials(1)
 
     angle = jnp.zeros((16, 128), F32)
     for i in range(3):
@@ -390,21 +404,21 @@
     key_new = turned(kv_new, base_c * ct - base_s * st, base_s * ct + base_c * st, lane)
     kn = jnp.where(lane < 64, key_new, kv_new).astype(BF16)
     vn = jnp.where(lane < 64, 1.0, kv_new).astype(BF16)
-    fresh_stats = jnp.zeros((16, 128), F32)
-    srow = iota((32, 16), 0)
-    scol = iota((32, 16), 1)
-    for i in range(3):
-        k = rank[3 * me + i]
-        q = q_all[k]
+    fresh_stats = [jnp.zeros((8, 128), F32)] * 2
+    srow = iota((16, 16), 0)
+    scol = iota((16, 16), 1)
+    for i, half in ((i, half) for i in range(3) for half in range(2)):
+        q = q_all[half * REQ + rank[3 * me + i]]
         seen = ((scol >> 2) == i) & ((scol & 3) <= (srow & 3))
         s = jnp.where(seen, dot(q, kn, NT), LOW)
         peak = jnp.max(s, axis=1, keepdims=True).astype(BF16).astype(F32)
         w = jnp.exp(s - peak).astype(BF16)
-        values, stats = tiles_of(dot(w, vn, NN), peak, lane)
-        rcv1[N_SEQ, 16 * i : 16 * i + 16, :] = values
-        fresh_stats = fresh_stats + (stats if i == 0 else pltpu.roll(stats, 8 * i, 1))
-    folded = fresh_stats[:8] + pltpu.roll(fresh_stats[8:], 64, 1)
-    rcv1[N_SEQ, 48:56, :] = folded.astype(BF16)
+        peak = jnp.broadcast_to(peak, (16, 128))
+        values, stats = tiles_of(dot(w, vn, NN), peak, lane8)
+        rcv1[half, N_SEQ, 8 * i : 8 * i + 8, :] = values
+        fresh_stats[half] = fresh_stats[half] + (stats if i == 0 else pltpu.roll(stats, 8 * i, 1))
+    for half in range(2):
+        rcv1[half, N_SEQ, 24:32, :] = fresh_stats[half].astype(BF16)
 
     sink = jnp.zeros((16, 128), F32)
     for j in range(8):
@@ -481,28 +495,27 @@
     gain_s[:, 2816:3072] = jnp.zeros((1, 256), F32)
     gain_s[:, 0:D] = gain[...]
 
-    others(N_SEQ, me, lambda s: seq_arrival(msg1, rcv1, send1, recv1, s).wait_recv())
-
-    stat_rows = rcv1[:, 48:56, :].reshape((N_SEQ + 1) * 8, 128)
     er = iota((128, 384), 0)
     ec = iota((128, 384), 1)
-    attended = []
-    for i in range(3):
-        for half in range(2):
-            spot = 64 * half + 8 * i + 4 * ((ec & 127) >> 6) + (ec >> 7)
-            expand = (er == spot).astype(F32).astype(BF16)
-            wide = dot(stat_rows, expand, NN)
+    expand = [
+        (er == 8 * i + 4 * ((ec & 127) >> 6) + (ec >> 7)).astype(F32).astype(BF16)
+        for i in range(3)
+    ]
+    for half in range(2):
+        others(N_SEQ, me, lambda o: seq_arrival(*exchange(half), o).wait_recv())
+        stat_rows = rcv1[half, :, 24:32, :].reshape((N_SEQ + 1) * 8, 128)
+        sunk = sink[8 * half : 8 * half + 8]
+        for i in range(3):
+            wide = dot(stat_rows, expand[i], NN)
             peaks = wide[:, 0:128].reshape(N_SEQ + 1, 8, 128)
             totals = (wide[:, 128:256] + wide[:, 256:384]).reshape(N_SEQ + 1, 8, 128)
-            sunk = sink[8 * half : 8 * half + 8]
             top = jnp.maximum(jnp.max(peaks, axis=0), sunk)
             factor = jnp.exp(peaks - top[None])
-            start = 16 * i + 8 * half
-            values = rcv1[:, start : start + 8, :].astype(F32)
+            values = rcv1[half, :, 8 * i : 8 * i + 8, :].astype(F32)
             num = jnp.sum(values * factor, axis=0)
             den = jnp.sum(totals * factor, axis=0) + jnp.exp(sunk - top)
-            attended.append(num / den)
-    att = jnp.concatenate(attended, axis=0).astype(BF16)
+            att_s[16 * i + 8 * half : 16 * i + 8 * half + 8, :] = num / den
+    att = att_s[...].astype(BF16)
     rr = iota((64, 48), 0)
     rc = iota((64, 48), 1)
     want = ((rr & 15) >> 2) * 16 + (rr >> 4) * 4 + (rr & 3)
@@ -634,7 +647,8 @@
             out_ref[i, :, j * CH : j * CH + width] = rcv7[j, 4 * i : 4 * i + 4, 0:width]
 
     for msg, rcv, send, recv in (
-        (msg1, rcv1, send1, recv1),
+        exchange(0),
+        exchange(1),
         (msg3, rcv3, send3, recv3),
         (msg6, rcv6, send6, recv6),
     ):
@@ -715,19 +729,20 @@
             pltpu.VMEM((REQ, 128), F32),
             pltpu.VMEM((REQ, 128), F32),
             pltpu.VMEM((16, 128), F32),
+            pltpu.VMEM((48, 128), F32),
             pltpu.VMEM((16, 128), F32),
             pltpu.VMEM((16, 3072), F32),
             pltpu.VMEM((ROWS, 2 * CH), F32),
             pltpu.VMEM((ROWS, 128), F32),
-            pltpu.VMEM((REQ, 32, 128), BF16),
-            pltpu.VMEM((MEMBERS * 32, PBLOCK + 128), F32),
-            pltpu.VMEM((MEMBERS * 32, PBLOCK + 128), F32),
-            pltpu.VMEM((MEMBERS * 32, 128), F32),
-            pltpu.VMEM((MEMBERS * 32, 128), F32),
-            pltpu.VMEM((REQ, 16, 128), BF16),
-            pltpu.VMEM((REQ, 16, 128), F32),
-            pltpu.VMEM((N_SEQ, 56, 128), BF16),
-            pltpu.VMEM((N_SEQ + 1, 56, 128), BF16),
+            pltpu.VMEM((2 * REQ, 16, 128), BF16),
+            pltpu.VMEM((MEMBERS * 16, PBLOCK + 128), F32),
+            pltpu.VMEM((MEMBERS * 16, PBLOCK + 128), F32),
+            pltpu.VMEM((MEMBERS * 16, 128), F32),
+            pltpu.VMEM((MEMBERS * 16, 128), F32),
+            pltpu.VMEM((2 * REQ, 8, 128), BF16),
+            pltpu.VMEM((2 * REQ, 8, 128), F32),
+            pltpu.VMEM((2, N_SEQ, 32, 128), BF16),
+            pltpu.VMEM((2, N_SEQ + 1, 32, 128), BF16),
             pltpu.VMEM((N_HEAD, 16, CH), BF16),
             pltpu.VMEM((N_HEAD, 16, CH), BF16),
             pltpu.VMEM((N_SEQ, 16, 128), BF16),
@@ -744,6 +759,8 @@
             pltpu.VMEM((N_HEAD, 16, CH), BF16),
             pltpu.SemaphoreType.DMA((6,)),
             pltpu.SemaphoreType.DMA((GROUPS,)),
+            seq_sem,
+            seq_sem,
             seq_sem,
             seq_sem,
             head_sem,

time: 81 us -> 81 us (level)
  no operation moved by 1% of the time
where the time goes in v5:
time: 81 us; the launch traced here: 80.8 us
  Pallas kernels  76.3 us (94%)
  local copies, waits for them, and re-layouts  2.86 us (4%)
  other arithmetic  1.55 us (2%)
    pallas_call x1, Pallas kernels, on_device(): pl.pallas_call(layer_kernel, name='layer', out_shape=jax.ShapeDtypeStruct...  76.3 us

profile of v5, /device:TPU:1, one launch (start us, length us, event | category | flops | bytes accessed | tf_op | source)
XLA Modules:
  0.0 80.8 jit_solution(17716405398562663609)
XLA Ops:
  0.0 0.9 %convert_reduce_fusion.rank = s32[96]{0:T(128)S(1)} fusion(s32[96]{0:T(128)} %prompt_group.1), kind=kLoop, calls=%fused_computation.2 | loop fusion | flops 64416 | bytes 768 | tf_op jit(solution)/shard_map/reduce_sum | solution.py:688
  0.9 0.0 copy-start
  0.9 0.6 select_reduce_fusion.order
  1.6 1.3 %reshape.18.gain = f32[1,2880]{1,0:T(1,128)} reshape(f32[2880]{0:T(1024)} %param.26) | data formatting | bytes 23040 | tf_op jit(solution)/shard_map/reshape | solution.py:699
  2.9 0.0 copy-done
  2.9 76.3 %layer.1 = bf16[3,4,2880]{2,1,0:T(4,128)(2,1)} custom-call(s32[96]{0:T(128)} %select_reduce_fusion.order, s32[96]{0:T(128)} %copy-done, s32[96]{0:T(128)} %prompt_group.1, s32[96]{0:T(128)} %tail_lens.1, s32[8]{0:T(128)} %prompt_lens.1, f32[8]{0:T(128)} %sinks.1, f32[40,128]{1,0:T(8,128)} %constant.4.clone.tables, bf16[3,4,128]{2,1,0:T(4,128)(2,1)} %bitcast.21, ...), custom_call_target="tpu_custom_call" | custom-call | tf_op jit(solution)/shard_map/layer/pallas_call | solution.py:713
  79.2 1.5 %copy.20 = bf16[3,4,2880]{2,1,0:T(4,128)(2,1)} copy(bf16[3,4,2880]{2,1,0:T(4,128)(2,1)} %layer.1) | data formatting | bytes 138240
Async XLA Ops:
  0.9 2.0 %copy-start = (s32[96]{0:T(128)}, s32[96]{0:T(128)S(1)}, u32[]{:S(2)}) copy-start(s32[96]{0:T(128)S(1)} %convert_reduce_fusion.rank) | copy-start | bytes 1156

commit v6 on v4

--- a/solution.py
+++ b/solution.py
@@ -194,8 +194,10 @@
     load_gate.start()
     load_up.start()
     load_dn.start()
-    lax.fori_loop(1, N_SEQ, greet_seq, 0)
-    lax.fori_loop(1, N_HEAD, greet_head, 0)
+    for d in range(1, N_SEQ):
+        greet_seq(d, 0)
+    for d in range(1, N_HEAD):
+        greet_head(d, 0)
 
     lane = iota((16, 128), 1)
     row = iota((16, 128), 0)
@@ -361,11 +363,8 @@
         )
 
     def others(count, mine, body):
-        def step(d, carry):
+        for d in range(1, count):
             body(lax.rem(mine + d, count))
-            return carry
-
-        lax.fori_loop(1, count, step, 0)
 
     core = lax.rem(head, 2)
     chip = head // 2
@@ -479,7 +478,7 @@
     gu_w[:, 2816:3072] = jnp.zeros((2 * CH, 256), BF16)
     gu_w[:, 0:D] = gu_v[...]
     gain_s[:, 2816:3072] = jnp.zeros((1, 256), F32)
-    gain_s[:, 0:D] = gain[...]
+    gain_s[:, 0:D] = gain[...].reshape(1, D)
 
     others(N_SEQ, me, lambda s: seq_arrival(msg1, rcv1, send1, recv1, s).wait_recv())
 
@@ -630,8 +629,7 @@
     others(N_HEAD, head, lambda s: head_arrival(msg7, None, rcv7, send7, recv7, s).wait_recv())
     for i in range(3):
         for j in range(N_HEAD):
-            width = CH if j < N_HEAD - 1 else LASTC
-            out_ref[i, :, j * CH : j * CH + width] = rcv7[j, 4 * i : 4 * i + 4, 0:width]
+            out_ref[i, :, j * CH : j * CH + CH] = rcv7[j, 4 * i : 4 * i + 4, :]
 
     for msg, rcv, send, recv in (
         (msg1, rcv1, send1, recv1),
@@ -682,7 +680,6 @@
     tables[24:40] = np.sin(step_angle)
     fresh = fresh_key_value.transpose(0, 2, 1, 3).reshape(3, 4, 128)
     ids = expert_ids.transpose(1, 2, 0)
-    gain = norm_gain.reshape(1, D)
     q = new_query.reshape(REQ, 4, 4, 128).transpose(0, 2, 1, 3).reshape(REQ, 16, 128)
     prompt = prompt_cache.transpose(0, 2, 1, 3).reshape(GROUPS, PBLOCK, 128)
     tail = decoded_tail_cache.transpose(0, 2, 1, 3).reshape(REQ, TBLOCK, 128)
@@ -699,7 +696,7 @@
     out = pl.pallas_call(
         layer_kernel,
         name="layer",
-        out_shape=jax.ShapeDtypeStruct((3, 4, D), BF16),
+        out_shape=jax.ShapeDtypeStruct((3, 4, 3072), BF16),
         in_specs=[smem] * 6 + [vmem] * 6 + [hbm] * 6,
         out_specs=vmem,
         scratch_shapes=[
@@ -777,7 +774,7 @@
         ids,
         route_weights,
         resid,
-        gain,
+        norm_gain,
         q,
         prompt,
         tail,
@@ -785,7 +782,7 @@
         gu,
         dn,
     )
-    return out
+    return out[:, :, :D]
 
 
 def solution(mesh):

time: 81 us -> 78 us (0.963)
  Pallas kernels: 76.4 us -> 74.8 us
  local copies, waits for them, and re-layouts: 2.86 us -> 1.55 us
    pallas_call x1, Pallas kernels: 76.4 us -> 74.8 us  [on_device(): pl.pallas_call(layer_kernel, name='layer', out_shape=jax.ShapeDtypeStruct...]
    slice x0 -> x1, local copies, waits for them, and re-layouts: none -> 1.54 us  [on_device(): return out[:, :, :D]]
    unnamed x3 -> x2, local copies, waits for them, and re-layouts: 1.54 us -> 0.01 us
    reshape x1 -> x0, local copies, waits for them, and re-layouts: 1.31 us -> none  [on_device(): gain = norm_gain.reshape(1, D)]
where the time goes in v6:
time: 78 us; the launch traced here: 77.9 us
  Pallas kernels  74.8 us (96%)
  local copies, waits for them, and re-layouts  1.55 us (2%)
  other arithmetic  1.54 us (2%)
    pallas_call x1, Pallas kernels, on_device(): pl.pallas_call(layer_kernel, name='layer', out_shape=jax.ShapeDtypeStruct...  74.8 us

profile of v6, /device:TPU:1, one launch (start us, length us, event | category | flops | bytes accessed | tf_op | source)
XLA Modules:
  0.0 77.9 jit_solution(6476776075505704808)
XLA Ops:
  0.0 0.9 %convert_reduce_fusion.rank = s32[96]{0:T(128)S(1)} fusion(s32[96]{0:T(128)} %prompt_group.1), kind=kLoop, calls=%fused_computation.2 | loop fusion | flops 64416 | bytes 768 | tf_op jit(solution)/shard_map/reduce_sum | solution.py:672
  0.9 0.0 copy-start
  0.9 0.6 select_reduce_fusion.order
  1.6 0.0 copy-done
  1.6 74.8 %layer.1 = bf16[3,4,3072]{2,1,0:T(4,128)(2,1)} custom-call(s32[96]{0:T(128)} %select_reduce_fusion.order, s32[96]{0:T(128)} %copy-done, s32[96]{0:T(128)} %prompt_group.1, s32[96]{0:T(128)} %tail_lens.1, s32[8]{0:T(128)} %prompt_lens.1, f32[8]{0:T(128)} %sinks.1, f32[40,128]{1,0:T(8,128)} %constant.4.clone.tables, bf16[3,4,128]{2,1,0:T(4,128)(2,1)} %bitcast.21, ...), custom_call_target="tpu_custom_call" | custom-call | tf_op jit(solution)/shard_map/layer/pallas_call | solution.py:696
  76.3 1.5 %slice.3 = bf16[3,4,2880]{2,1,0:T(4,128)(2,1)} slice(bf16[3,4,3072]{2,1,0:T(4,128)(2,1)} %layer.1), slice={[0:3], [0:4], [0:2880]} | slice | bytes 138240 | tf_op jit(solution)/shard_map/slice | solution.py:785
Async XLA Ops:
  0.9 0.6 copy-start

commit v7 on v6

--- a/solution.py
+++ b/solution.py
@@ -30,6 +30,12 @@
 NT = (((1,), (1,)), ((), ()))
 NN = (((1,), (0,)), ((), ()))
 TN = (((0,), (0,)), ((), ()))
+
+
+SEQ_ORDER = sorted(
+    ((dy, dz) for dy in range(4) for dz in range(8) if dy or dz),
+    key=lambda o: (-min(o[0], 4 - o[0]) - min(o[1], 8 - o[1]), (o[0] * 3 + o[1] * 5) % 8),
+)
 
 
 def dot(a, b, dims):
@@ -311,6 +317,8 @@
 
     lax.fori_loop(0, GROUPS // 2, two_groups, 0)
 
+    rcv3[...] = jnp.zeros((N_SEQ, 16, 128), BF16)
+    rcv6[...] = jnp.zeros((N_SEQ, 16, 128), BF16)
     pl.semaphore_wait(barrier, N_SEQ - 1 + N_HEAD - 1)
 
     def pack(dst, slot, o):
@@ -323,9 +331,10 @@
         dst[slot, 48:56, :] = (total[:8] + pltpu.roll(total[8:], 64, 1)).astype(BF16)
 
     def seq_copy(msg, rcv, send, recv, to):
+        rows = 56 if msg is msg1 else 10
         return pltpu.make_async_remote_copy(
-            src_ref=msg.at[to],
-            dst_ref=rcv.at[me],
+            src_ref=msg.at[to, pl.ds(0, rows)],
+            dst_ref=rcv.at[me, pl.ds(0, rows)],
             send_sem=send.at[to],
             recv_sem=recv.at[me],
             device_id=(to, head),
@@ -333,9 +342,10 @@
         )
 
     def seq_arrival(msg, rcv, send, recv, source):
+        rows = 56 if msg is msg1 else 10
         return pltpu.make_async_remote_copy(
-            src_ref=msg.at[source],
-            dst_ref=rcv.at[source],
+            src_ref=msg.at[source, pl.ds(0, rows)],
+            dst_ref=rcv.at[source, pl.ds(0, rows)],
             send_sem=send.at[source],
             recv_sem=recv.at[source],
             device_id=(source, head),
@@ -363,14 +373,22 @@
         )
 
     def others(count, mine, body):
-        for d in range(1, count):
-            body(lax.rem(mine + d, count))
+        if count == N_HEAD:
+            for j in head_order:
+                body(j)
+        else:
+            for dy, dz in SEQ_ORDER:
+                body(lax.rem(me // 8 + dy, 4) * 8 + lax.rem(lax.rem(me, 8) + dz, 8))
 
     core = lax.rem(head, 2)
     chip = head // 2
     near = chip + 1 - 2 * lax.rem(chip, 2)
     sibling = 2 * chip + 1 - core
     far = [near, 3 - chip, lax.rem(chip + 2, 4)]
+    head_order = []
+    for c in (far[2], far[0], far[1]):
+        head_order += [2 * c + core, 2 * c + 1 - core]
+    head_order.append(sibling)
 
     def send_partials(o):
         pack(msg1, o, o)

time: 78 us -> 74.2 us (0.951)
  Pallas kernels: 74.8 us -> 70.9 us
    pallas_call x1, Pallas kernels: 74.8 us -> 70.9 us  [on_device(): pl.pallas_call(layer_kernel, name='layer', out_shape=jax.ShapeDtypeStruct...]
where the time goes in v7:
time: 74.2 us; the launch traced here: 74 us
  Pallas kernels  70.9 us (96%)
  local copies, waits for them, and re-layouts  1.55 us (2%)
  other arithmetic  1.54 us (2%)
    pallas_call x1, Pallas kernels, on_device(): pl.pallas_call(layer_kernel, name='layer', out_shape=jax.ShapeDtypeStruct...  70.9 us
    slice x1, local copies, waits for them, and re-layouts, on_device(): return out[:, :, :D]  1.54 us

profile of v7, /device:TPU:1, one launch (start us, length us, event | category | flops | bytes accessed | tf_op | source)
XLA Modules:
  0.0 74.0 jit_solution(4382196581275608194)
XLA Ops:
  0.0 0.9 %convert_reduce_fusion.rank = s32[96]{0:T(128)S(1)} fusion(s32[96]{0:T(128)} %prompt_group.1), kind=kLoop, calls=%fused_computation.2 | loop fusion | flops 64416 | bytes 768 | tf_op jit(solution)/shard_map/reduce_sum | solution.py:690
  0.9 0.0 copy-start
  0.9 0.6 select_reduce_fusion.order
  1.6 0.0 copy-done
  1.6 70.9 %layer.1 = bf16[3,4,3072]{2,1,0:T(4,128)(2,1)} custom-call(s32[96]{0:T(128)} %select_reduce_fusion.order, s32[96]{0:T(128)} %copy-done, s32[96]{0:T(128)} %prompt_group.1, s32[96]{0:T(128)} %tail_lens.1, s32[8]{0:T(128)} %prompt_lens.1, f32[8]{0:T(128)} %sinks.1, f32[40,128]{1,0:T(8,128)} %constant.4.clone.tables, bf16[3,4,128]{2,1,0:T(4,128)(2,1)} %bitcast.21, ...), custom_call_target="tpu_custom_call" | custom-call | tf_op jit(solution)/shard_map/layer/pallas_call | solution.py:714
  72.4 1.5 %slice.3 = bf16[3,4,2880]{2,1,0:T(4,128)(2,1)} slice(bf16[3,4,3072]{2,1,0:T(4,128)(2,1)} %layer.1), slice={[0:3], [0:4], [0:2880]} | slice | bytes 138240 | tf_op jit(solution)/shard_map/slice | solution.py:803
Async XLA Ops:
  0.9 0.6 copy-start

commit v8 on v7

--- a/solution.py
+++ b/solution.py
@@ -259,23 +259,23 @@
         kv = prompt_v[g]
         bias = jnp.where(key_col < prompt_lens[g], 0.0, LOW)
         q = q_all[pl.ds(g * MEMBERS, MEMBERS)].reshape(MEMBERS * 32, 128)
-        high = None
-        for h in range(4):
-            cols = slice(256 * h, 256 * h + 256)
-            part = dot(q, kv[cols], NT) + bias[:, cols]
-            buf[:, cols] = part
-            part = jnp.maximum(part[:, :128], part[:, 128:])
-            high = part if high is None else jnp.maximum(high, part)
         keys, members = tails(g)
         for b in range(3):
             rows = slice(128 * b, 128 * b + 128)
+            high = None
+            for h in range(4):
+                cols = slice(256 * h, 256 * h + 256)
+                part = dot(q[rows], kv[cols], NT) + bias[:, cols]
+                buf[rows, cols] = part
+                part = jnp.maximum(part[:, :128], part[:, 128:])
+                high = part if high is None else jnp.maximum(high, part)
             limit = jnp.zeros((1, 128), jnp.int32)
             for i in range(4):
                 limit = jnp.where((col128 >> 5) == i, tail_lens[members[4 * b + i]], limit)
             seen = same_req & (((col128 & 31) + me * TBLOCK) < limit)
             part = jnp.where(seen, dot(q[rows], keys[b], NT), LOW)
             buf[rows, PBLOCK : PBLOCK + 128] = part
-            top = jnp.max(jnp.maximum(high[rows], part), axis=1, keepdims=True)
+            top = jnp.max(jnp.maximum(high, part), axis=1, keepdims=True)
             top = jnp.maximum(top, FLOOR).astype(BF16).astype(F32)
             tops[rows, :] = jnp.broadcast_to(top, (128, 128))
 
@@ -546,6 +546,8 @@
     msg3[...] = dot(select, hidden_rows, NN).astype(BF16).reshape(N_SEQ, 16, 128)
     others(N_SEQ, me, lambda o: seq_copy(msg3, rcv3, send3, recv3, o).start())
     rcv3[me] = msg3[me]
+    others(N_SEQ, me, lambda o: seq_copy(msg1, rcv1, send1, recv1, o).wait_send())
+    others(N_HEAD, head, lambda o: head_copy(msg2, o, rcv2, send2, recv2, o).wait_send())
     others(N_SEQ, me, lambda s: seq_arrival(msg3, rcv3, send3, recv3, s).wait_recv())
     got = dot(spread, rcv3[...].reshape(512, 128), NN).astype(BF16)
     mine = jnp.concatenate([got[96 * c : 96 * c + 96] for c in range(3)], axis=1)
@@ -636,6 +638,15 @@
     msg6[...] = dot(gather, summed_rows, NN).astype(BF16).reshape(N_SEQ, 16, 128)
     others(N_SEQ, me, lambda o: seq_copy(msg6, rcv6, send6, recv6, o).start())
     rcv6[me] = msg6[me]
+    others(N_SEQ, me, lambda o: seq_copy(msg3, rcv3, send3, recv3, o).wait_send())
+    for j in gather_to:
+        head_copy(msg4, None, rcv4, send4, recv4, j).wait_send()
+    for k in range(3):
+        forward(k, 2 * far[k] + core).wait_send()
+    for k, c in enumerate(turns):
+        pair_copy(c).wait_send()
+        if k < 3:
+            chip_copy(c, chip).wait_send()
     others(N_SEQ, me, lambda s: seq_arrival(msg6, rcv6, send6, recv6, s).wait_recv())
     back = rcv6[...].reshape(512, 128)
     added = dot(give_hi, back, NN) + dot(give_lo, back, NN)
@@ -644,26 +655,12 @@
     msg7[...] = result
     others(N_HEAD, head, lambda o: head_copy(msg7, None, rcv7, send7, recv7, o).start())
     rcv7[head] = result
+    others(N_SEQ, me, lambda o: seq_copy(msg6, rcv6, send6, recv6, o).wait_send())
     others(N_HEAD, head, lambda s: head_arrival(msg7, None, rcv7, send7, recv7, s).wait_recv())
     for i in range(3):
         for j in range(N_HEAD):
             out_ref[i, :, j * CH : j * CH + CH] = rcv7[j, 4 * i : 4 * i + 4, :]
 
-    for msg, rcv, send, recv in (
-        (msg1, rcv1, send1, recv1),
-        (msg3, rcv3, send3, recv3),
-        (msg6, rcv6, send6, recv6),
-    ):
-        others(N_SEQ, me, lambda o: seq_copy(msg, rcv, send, recv, o).wait_send())
-    for j in gather_to:
-        head_copy(msg4, None, rcv4, send4, recv4, j).wait_send()
-    for k in range(3):
-        forward(k, 2 * far[k] + core).wait_send()
-    for k, c in enumerate(turns):
-        pair_copy(c).wait_send()
-        if k < 3:
-            chip_copy(c, chip).wait_send()
-    others(N_HEAD, head, lambda o: head_copy(msg2, o, rcv2, send2, recv2, o).wait_send())
     others(N_HEAD, head, lambda o: head_copy(msg7, None, rcv7, send7, recv7, o).wait_send())
 
 

time: 74.2 us -> 73.7 us (level)
  no operation moved by 1% of the time
where the time goes in v8:
time: 73.7 us; the launch traced here: 73.5 us
  Pallas kernels  70.4 us (96%)
  local copies, waits for them, and re-layouts  1.55 us (2%)
  other arithmetic  1.54 us (2%)
    pallas_call x1, Pallas kernels, on_device(): pl.pallas_call(layer_kernel, name='layer', out_shape=jax.ShapeDtypeStruct...  70.4 us
    slice x1, local copies, waits for them, and re-layouts, on_device(): return out[:, :, :D]  1.54 us

profile of v8, /device:TPU:1, one launch (start us, length us, event | category | flops | bytes accessed | tf_op | source)
XLA Modules:
  0.0 73.5 jit_solution(2627955947149225678)
XLA Ops:
  0.0 0.9 %convert_reduce_fusion.rank = s32[96]{0:T(128)S(1)} fusion(s32[96]{0:T(128)} %prompt_group.1), kind=kLoop, calls=%fused_computation.2 | loop fusion | flops 64416 | bytes 768 | tf_op jit(solution)/shard_map/reduce_sum | solution.py:687
  0.9 0.0 copy-start
  0.9 0.6 select_reduce_fusion.order
  1.6 0.0 copy-done
  1.6 70.4 %layer.1 = bf16[3,4,3072]{2,1,0:T(4,128)(2,1)} custom-call(s32[96]{0:T(128)} %select_reduce_fusion.order, s32[96]{0:T(128)} %copy-done, s32[96]{0:T(128)} %prompt_group.1, s32[96]{0:T(128)} %tail_lens.1, s32[8]{0:T(128)} %prompt_lens.1, f32[8]{0:T(128)} %sinks.1, f32[40,128]{1,0:T(8,128)} %constant.4.clone.tables, bf16[3,4,128]{2,1,0:T(4,128)(2,1)} %bitcast.21, ...), custom_call_target="tpu_custom_call" | custom-call | tf_op jit(solution)/shard_map/layer/pallas_call | solution.py:711
  72.0 1.5 %slice.3 = bf16[3,4,2880]{2,1,0:T(4,128)(2,1)} slice(bf16[3,4,3072]{2,1,0:T(4,128)(2,1)} %layer.1), slice={[0:3], [0:4], [0:2880]} | slice | bytes 138240 | tf_op jit(solution)/shard_map/slice | solution.py:800
Async XLA Ops:
  0.9 0.6 copy-start

commit v9 on v8

--- a/solution.py
+++ b/solution.py
@@ -239,7 +239,7 @@
         ).astype(BF16)
         return carry
 
-    lax.fori_loop(0, REQ, rotate_one, 0, unroll=4)
+    lax.fori_loop(0, REQ, rotate_one, 0, unroll=8)
     load_tail.wait()
 
     key_col = iota((1, PBLOCK), 1) + me * PBLOCK
@@ -311,11 +311,14 @@
         g = 2 * k
         scores(g + 1, odd_s, odd_top)
         weigh(g, even_s, even_top)
-        scores(jnp.minimum(g + 2, GROUPS - 1), even_s, even_top)
+        scores(g + 2, even_s, even_top)
         weigh(g + 1, odd_s, odd_top)
         return carry
 
-    lax.fori_loop(0, GROUPS // 2, two_groups, 0)
+    lax.fori_loop(0, GROUPS // 2 - 1, two_groups, 0)
+    scores(GROUPS - 1, odd_s, odd_top)
+    weigh(GROUPS - 2, even_s, even_top)
+    weigh(GROUPS - 1, odd_s, odd_top)
 
     rcv3[...] = jnp.zeros((N_SEQ, 16, 128), BF16)
     rcv6[...] = jnp.zeros((N_SEQ, 16, 128), BF16)

time: 73.7 us -> 72.4 us (0.982)
  Pallas kernels: 70.4 us -> 69.1 us
    pallas_call x1, Pallas kernels: 70.4 us -> 69.1 us  [on_device(): pl.pallas_call(layer_kernel, name='layer', out_shape=jax.ShapeDtypeStruct...]
where the time goes in v9:
time: 72.4 us; the launch traced here: 72.2 us
  Pallas kernels  69.1 us (95%)
  local copies, waits for them, and re-layouts  1.55 us (2%)
  other arithmetic  1.54 us (2%)
    pallas_call x1, Pallas kernels, on_device(): pl.pallas_call(layer_kernel, name='layer', out_shape=jax.ShapeDtypeStruct...  69.1 us
    slice x1, local copies, waits for them, and re-layouts, on_device(): return out[:, :, :D]  1.54 us

profile of v9, /device:TPU:1, one launch (start us, length us, event | category | flops | bytes accessed | tf_op | source)
XLA Modules:
  0.0 72.2 jit_solution(15632397112922282714)
XLA Ops:
  0.0 0.9 %convert_reduce_fusion.rank = s32[96]{0:T(128)S(1)} fusion(s32[96]{0:T(128)} %prompt_group.1), kind=kLoop, calls=%fused_computation.2 | loop fusion | flops 64416 | bytes 768 | tf_op jit(solution)/shard_map/reduce_sum | solution.py:690
  0.9 0.0 copy-start
  0.9 0.6 select_reduce_fusion.order
  1.6 0.0 copy-done
  1.6 69.1 %layer.1 = bf16[3,4,3072]{2,1,0:T(4,128)(2,1)} custom-call(s32[96]{0:T(128)} %select_reduce_fusion.order, s32[96]{0:T(128)} %copy-done, s32[96]{0:T(128)} %prompt_group.1, s32[96]{0:T(128)} %tail_lens.1, s32[8]{0:T(128)} %prompt_lens.1, f32[8]{0:T(128)} %sinks.1, f32[40,128]{1,0:T(8,128)} %constant.4.clone.tables, bf16[3,4,128]{2,1,0:T(4,128)(2,1)} %bitcast.21, ...), custom_call_target="tpu_custom_call" | custom-call | tf_op jit(solution)/shard_map/layer/pallas_call | solution.py:714
  70.6 1.5 %slice.3 = bf16[3,4,2880]{2,1,0:T(4,128)(2,1)} slice(bf16[3,4,3072]{2,1,0:T(4,128)(2,1)} %layer.1), slice={[0:3], [0:4], [0:2880]} | slice | bytes 138240 | tf_op jit(solution)/shard_map/slice | solution.py:803
Async XLA Ops:
  0.9 0.6 copy-start
